TPU v7x, 256 devices: a whole 4x4x8 slice. The times are simulated.
256 devices in a mesh: azim: 16 (over x_lo, z), cross: 8 (over x_hi, y), role: 2 (over core).
Axes of the slice: x: 4 (x_hi: 2, x_lo: 2; x = x_hi * 2 + x_lo), y: 4, z: 8, core: 2. Of those that a mesh axis runs over, the one named last changes fastest.
Arguments:
- checkpoint: float32 [8, 16, 32, 2048], P(None, ('cross', 'role'), None, 'azim'), may hold values from -1.2 to 8.1, as said below
- primary_arrhenius_exponent: float32 [16, 32, 2048], P(('cross', 'role'), None, 'azim'), may hold values from 0 to 2.3
- cell_types: int32 [16, 32, 2048], P(('cross', 'role'), None, 'azim'), may hold values from 0 to 2
- final_adjoint: float32 [8, 16, 32, 2048], P(None, None, ('cross', 'role'), 'azim'), may hold values from -6 to 6
Outputs:
- adjoint_start: float32 [8, 16, 32, 2048], P(None, None, ('cross', 'role'), 'azim')
- rate_gradient: float32 [16, 32, 2048], P(None, ('cross', 'role'), 'azim')
Inputs may be any that keep to these rules, and one draw needn't show every extreme that they name: `checkpoint`: density lies between 0.7 and 1.4 and pressure between 0.35 and 2 in every cell; fuel, radical and product densities are nonnegative and at most the density.
All inputs are finite; a program needn't handle non-finite values.
Results may differ from a plain program's by a relative error of at most 0.0003.
Values sent between devices are 32-bit elements; how exact they have to be, the bound alone decides.
No kernel may reach another device: no remote copies, remote signals or barrier semaphores. Data moves between devices by JAX's collectives and lax.ppermute only.
A program may use at most 64 MiB of HBM per device.

v0:
```python
import jax
import jax.numpy as jnp
from jax import lax
from jax.sharding import PartitionSpec as P

HEAT_RATIO = 1.3
WAVE_SPEED = 4.0
TIME_STEP = 0.06
PRIMARY_BARRIER = 1.0
SECONDARY_ENERGY = 1.5
SECONDARY_SCALE = 2.0
HEAT_FIRST = 3.0
HEAT_SECOND = 2.0
INJECT_RELAX = 2.0
SPONGE_RELAX = 1.0
FRESH_STATE = (1.0, 0.8, 0.0, 0.0, 1.0 / (HEAT_RATIO - 1.0) + 0.32, 1.0, 0.0, 0.0)
DAMPED_ROWS = (0.0, 1.0, 1.0, 1.0, 0.0, 0.0, 0.0, 0.0)


def extended(cells, sides, width, closed):
    for axis, dim in sides:
        count = lax.axis_size(axis)
        ends = count if closed else count - 1
        head = lax.slice_in_dim(cells, 0, width, axis=dim)
        tail = lax.slice_in_dim(cells, cells.shape[dim] - width, cells.shape[dim], axis=dim)
        cells = jnp.concatenate(
            [
                lax.ppermute(tail, axis, [(i, (i + 1) % count) for i in range(ends)]),
                cells,
                lax.ppermute(head, axis, [((i + 1) % count, i) for i in range(ends)]),
            ],
            axis=dim,
        )
    return cells


def padded_2(shard, sides, width):
    edges = {}
    for axis, dim in sides:
        peers, length = (lax.axis_size(axis), shard.shape[dim])
        up = [(i, (i + 1) % peers) for i in range(peers - 1)]
        last = lax.slice_in_dim(shard, length - width, length, axis=dim)
        first = lax.slice_in_dim(shard, 0, width, axis=dim)
        edges[dim] = (
            lax.ppermute(last, axis, up),
            lax.ppermute(first, axis, [(b, a) for a, b in up]),
        )
    done = []
    for _, dim in sides:
        low, high = edges[dim]
        around = [(width, width) if d in done else (0, 0) for d in range(shard.ndim)]
        shard = jnp.concatenate([jnp.pad(low, around), shard, jnp.pad(high, around)], axis=dim)
        done.append(dim)
    return shard


def side_by_side(arrays, axis, split_dim, concat_dim, along):
    ends, at = ([], 0)
    for a in arrays[:-1]:
        at += a.shape[along]
        ends.append(at)
    both = jnp.concatenate(arrays, axis=along)
    return tuple(
        jnp.split(
            lax.all_to_all(both, axis, split_axis=split_dim, concat_axis=concat_dim, tiled=True),
            ends,
            axis=along,
        )
    )


def cell_flux(fields, which_axis):
    volumetric_weight = fields[0]
    velocity = fields[which_axis] / volumetric_weight
    thermodynamic_stress = (HEAT_RATIO - 1.0) * (
        fields[4]
        - 0.5
        * (fields[1] * fields[1] + fields[2] * fields[2] + fields[3] * fields[3])
        / volumetric_weight
    )
    carried = fields * velocity[None]
    carried = carried.at[which_axis].add(thermodynamic_stress)
    carried = carried.at[4].add(thermodynamic_stress * velocity)
    return carried


def flux_difference(fields, which_axis):
    count = fields.shape[which_axis]
    values = cell_flux(fields, which_axis)
    lower_values = lax.slice_in_dim(values, 0, count - 1, axis=which_axis)
    upper_values = lax.slice_in_dim(values, 1, count, axis=which_axis)
    lower_fields = lax.slice_in_dim(fields, 0, count - 1, axis=which_axis)
    upper_fields = lax.slice_in_dim(fields, 1, count, axis=which_axis)
    face_flux = 0.5 * (lower_values + upper_values) - 0.5 * WAVE_SPEED * (
        upper_fields - lower_fields
    )
    return lax.slice_in_dim(face_flux, 1, count - 1, axis=which_axis) - lax.slice_in_dim(
        face_flux, 0, count - 2, axis=which_axis
    )


def section_update(padded, primary_arrhenius_exponent, cell_kinds):
    divergence = flux_difference(padded[:, :, 1:-1, 1:-1], 1)
    divergence = divergence + flux_difference(padded[:, 1:-1, :, 1:-1], 2)
    divergence = divergence + flux_difference(padded[:, 1:-1, 1:-1, :], 3)
    middle_volumes = padded[:, 1:-1, 1:-1, 1:-1]
    volumetric_weight = middle_volumes[0]
    thermodynamic_stress = (HEAT_RATIO - 1.0) * (
        middle_volumes[4]
        - 0.5
        * (
            middle_volumes[1] * middle_volumes[1]
            + middle_volumes[2] * middle_volumes[2]
            + middle_volumes[3] * middle_volumes[3]
        )
        / volumetric_weight
    )
    thermal_kelvin = thermodynamic_stress / volumetric_weight
    primary_reaction_speed = (
        jnp.exp(primary_arrhenius_exponent - PRIMARY_BARRIER / thermal_kelvin) * middle_volumes[5]
    )
    secondary_reaction_speed = (
        SECONDARY_SCALE * jnp.exp(-SECONDARY_ENERGY / thermal_kelvin) * middle_volumes[6]
    )
    nothing = jnp.zeros_like(primary_reaction_speed)
    reaction = jnp.stack(
        [
            nothing,
            nothing,
            nothing,
            nothing,
            HEAT_FIRST * primary_reaction_speed + HEAT_SECOND * secondary_reaction_speed,
            -primary_reaction_speed,
            primary_reaction_speed - secondary_reaction_speed,
            secondary_reaction_speed,
        ]
    )
    inject = jnp.where(cell_kinds == 1.0, 1.0, 0.0).astype(middle_volumes.dtype)
    sponge = jnp.where(cell_kinds == 2.0, 1.0, 0.0).astype(middle_volumes.dtype)
    fresh = jnp.array(FRESH_STATE, dtype=middle_volumes.dtype).reshape(8, 1, 1, 1)
    damped = jnp.array(DAMPED_ROWS, dtype=middle_volumes.dtype).reshape(8, 1, 1, 1)
    source = (
        reaction
        + INJECT_RELAX * inject[None] * (fresh - middle_volumes)
        - SPONGE_RELAX * sponge[None] * damped * middle_volumes
    )
    return middle_volumes + TIME_STEP * (source - divergence)


def fix_edges(widened, which_axis, at_first, at_last):
    count = widened.shape[which_axis]
    first_row = lax.slice_in_dim(widened, 0, 1, axis=which_axis)
    second_row = lax.slice_in_dim(widened, 1, 2, axis=which_axis)
    before_last = lax.slice_in_dim(widened, count - 2, count - 1, axis=which_axis)
    last_row = lax.slice_in_dim(widened, count - 1, count, axis=which_axis)
    middle = lax.slice_in_dim(widened, 1, count - 1, axis=which_axis)
    return jnp.concatenate(
        [
            jnp.where(at_first, second_row, first_row),
            middle,
            jnp.where(at_last, before_last, last_row),
        ],
        axis=which_axis,
    )


def local_update(surrounded, rate_here, kinds_here, at_first, at_last):
    fixed = fix_edges(surrounded, 2, at_first, at_last)
    padded = jnp.pad(fixed, ((0, 0), (1, 1), (0, 0), (0, 0)), mode="edge")
    return section_update(padded, rate_here, kinds_here)


def return_ghosts(cot_surrounded):
    middle = cot_surrounded[:, :, 1:-1, :]
    edges = jnp.concatenate([middle[..., :1], middle[..., -1:]], axis=3)
    arrived = extended(edges, (("azim", 3),), 1, True)
    interior = middle[..., 1:-1]
    interior = interior.at[..., 0].add(arrived[..., 0])
    interior = interior.at[..., -1].add(arrived[..., 3])
    rims = jnp.concatenate(
        [cot_surrounded[:, :, :1, 1:-1], cot_surrounded[:, :, -1:, 1:-1]], axis=2
    )
    landed = extended(rims, ((("cross", "role"), 2),), 1, False)
    interior = interior.at[:, :, 0].add(landed[:, :, 0])
    interior = interior.at[:, :, -1].add(landed[:, :, 3])
    return interior


def shards(checkpoint, primary_arrhenius_exponent, cell_types, final_adjoint):
    position = lax.axis_index(("cross", "role"))
    at_first = position == 0
    at_last = position == lax.axis_size(("cross", "role")) - 1
    kinds_forward = cell_types.astype(jnp.float32)
    extras = jnp.stack([primary_arrhenius_exponent, kinds_forward])

    def rebuild(fields):
        widened = extended(fields, (("azim", 3),), 1, True)
        return padded_2(widened, ((("cross", "role"), 2),), 1)

    start_state, extra_relayed = side_by_side((checkpoint, extras), ("cross", "role"), 2, 1, 0)
    rate_adjoint = extra_relayed[0]
    kinds_adjoint = extra_relayed[1]
    held_zero = rebuild(start_state)
    state_one = local_update(held_zero, rate_adjoint, kinds_adjoint, at_first, at_last)
    held_one = rebuild(state_one)
    state_two = 0.5 * start_state + 0.5 * local_update(
        held_one, rate_adjoint, kinds_adjoint, at_first, at_last
    )
    held_two = rebuild(state_two)
    state_three = local_update(held_two, rate_adjoint, kinds_adjoint, at_first, at_last)
    held_three = rebuild(state_three)
    surrounded = [held_zero, held_one, held_two, held_three]

    def back_section(held_state, cotangent):

        def local(held_in, rate_in):
            return local_update(held_in, rate_in, kinds_adjoint, at_first, at_last)

        unused, pullback = jax.vjp(local, held_state, rate_adjoint)
        cot_held, cot_rate = pullback(cotangent)
        return (return_ghosts(cot_held), cot_rate)

    cot_three, grad_three = back_section(surrounded[3], 0.5 * final_adjoint)
    cot_back, grad_two = back_section(surrounded[2], cot_three)
    cot_two = 0.5 * final_adjoint + cot_back
    cot_one, grad_one = back_section(surrounded[1], 0.5 * cot_two)
    cot_first, grad_zero = back_section(surrounded[0], cot_one)
    adjoint_start = 0.5 * cot_two + cot_first
    rate_gradient = grad_three + grad_two + grad_one + grad_zero
    return (adjoint_start, rate_gradient)


def solution(mesh):
    return jax.shard_map(
        shards,
        mesh=mesh,
        in_specs=(
            P(None, ("cross", "role"), None, "azim"),
            P(("cross", "role"), None, "azim"),
            P(("cross", "role"), None, "azim"),
            P(None, None, ("cross", "role"), "azim"),
        ),
        out_specs=(P(None, None, ("cross", "role"), "azim"), P(None, ("cross", "role"), "azim")),
        check_vma=False,
    )
```

profile of v0, /device:TPU:6, one launch (start us, length us, event | category | flops | bytes accessed | tf_op | source)
XLA Modules:
  0.0 228.1 jit_solution(3839218811524174597)
XLA Ops:
  1.4 0.9 pad_maximum_fusion.59
  3.1 7.6 %all-to-all-start = ((f32[10,1,32,128]{3,0,1,2:T(8,128)}), f32[10,1,32,128]{3,0,1,2:T(8,128)S(1)}, u32[]{:S(2)}, u32[]{:S(2)}) async-start(f32[10,1,32,128]{3,0,1,2:T(8,128)} %copy.47), calls=%async_computation | async-start | bytes 524288 | tf_op jit(solution)/shard_map/all_to_all | solution.py:65
  10.8 6.7 %all-to-all-done = f32[10,1,32,128]{3,0,1,2:T(8,128)S(1)} async-done(((f32[10,1,32,128]{3,0,1,2:T(8,128)}), f32[10,1,32,128]{3,0,1,2:T(8,128)S(1)}, u32[]{:S(2)}, u32[]{:S(2)}) %all-to-all-start) | async-done | bytes 163872 | tf_op jit(solution)/shard_map/all_to_all | solution.py:65
  18.4 2.0 collective-permute-start
  20.4 4.3 %collective-permute-start.1 = (f32[8,16,2,1]{3,1,2,0:T(8,128)S(1)}, f32[8,16,2,1]{3,1,2,0:T(8,128)S(1)}, u32[]{:S(2)}, u32[]{:S(2)}) collective-permute-start(f32[8,16,2,1]{3,1,2,0:T(8,128)S(1)} %get-tuple-element.701), channel_id=1, source_target_pairs={{16,0},{32,16},{48,32},{64,48},{80,64},{96,80},{112,96},{128,112},... | collective-permute-start | bytes 3080 | tf_op jit(solution)/shard_map/ppermute | solution.py:30
  26.0 2.3 collective-permute-done
  28.5 1.9 collective-permute-start.2
  30.4 7.3 %collective-permute-start.3 = (f32[8,16,1,130]{3,1,2,0:T(8,128)S(1)}, f32[8,16,1,130]{3,1,2,0:T(8,128)S(1)}, u32[]{:S(2)}, u32[]{:S(2)}) collective-permute-start(f32[8,16,1,130]{3,1,2,0:T(8,128)S(1)} %get-tuple-element.673), channel_id=1, source_target_pairs={{1,0},{2,1},{3,2},{4,3},{5,4},{6,5},{7,6},{8,7},{9,8},{10,9},{11,1... | collective-permute-start | bytes 199688 | tf_op jit(solution)/shard_map/ppermute | solution.py:46
  38.7 1.5 collective-permute-done.3
  46.5 4.1 %collective-permute-start.5 = (f32[8,16,2,1]{3,1,2,0:T(8,128)S(1)}, f32[8,16,2,1]{3,1,2,0:T(8,128)S(1)}, u32[]{:S(2)}, u32[]{:S(2)}) collective-permute-start(f32[8,16,2,1]{3,1,2,0:T(8,128)S(1)} %get-tuple-element.699), channel_id=1, source_target_pairs={{16,0},{32,16},{48,32},{64,48},{80,64},{96,80},{112,96},{128,112},... | collective-permute-start | bytes 3080 | tf_op jit(solution)/shard_map/ppermute | solution.py:30
  50.7 2.9 %collective-permute-done.4 = f32[8,16,2,1]{3,1,2,0:T(8,128)S(1)} collective-permute-done((f32[8,16,2,1]{3,1,2,0:T(8,128)S(1)}, f32[8,16,2,1]{3,1,2,0:T(8,128)S(1)}, u32[]{:S(2)}, u32[]{:S(2)}) %collective-permute-start.4) | collective-permute-done | bytes 1056 | tf_op jit(solution)/shard_map/ppermute | solution.py:28
  53.9 1.9 collective-permute-start.6
  55.8 7.3 %collective-permute-start.7 = (f32[8,16,1,130]{3,1,2,0:T(8,128)S(1)}, f32[8,16,1,130]{3,1,2,0:T(8,128)S(1)}, u32[]{:S(2)}, u32[]{:S(2)}) collective-permute-start(f32[8,16,1,130]{3,1,2,0:T(8,128)S(1)} %get-tuple-element.669), channel_id=1, source_target_pairs={{1,0},{2,1},{3,2},{4,3},{5,4},{6,5},{7,6},{8,7},{9,8},{10,9},{11,1... | collective-permute-start | bytes 199688 | tf_op jit(solution)/shard_map/ppermute | solution.py:46
  64.1 1.5 collective-permute-done.7
  71.5 1.3 collective-permute-start.8
  72.8 2.8 %collective-permute-start.9 = (f32[8,16,2,1]{3,1,2,0:T(8,128)S(1)}, f32[8,16,2,1]{3,1,2,0:T(8,128)S(1)}, u32[]{:S(2)}, u32[]{:S(2)}) collective-permute-start(f32[8,16,2,1]{3,1,2,0:T(8,128)S(1)} %get-tuple-element.697), channel_id=1, source_target_pairs={{16,0},{32,16},{48,32},{64,48},{80,64},{96,80},{112,96},{128,112},... | collective-permute-start | bytes 3080 | tf_op jit(solution)/shard_map/ppermute | solution.py:30
  75.7 2.9 %collective-permute-done.8 = f32[8,16,2,1]{3,1,2,0:T(8,128)S(1)} collective-permute-done((f32[8,16,2,1]{3,1,2,0:T(8,128)S(1)}, f32[8,16,2,1]{3,1,2,0:T(8,128)S(1)}, u32[]{:S(2)}, u32[]{:S(2)}) %collective-permute-start.8) | collective-permute-done | bytes 1056 | tf_op jit(solution)/shard_map/ppermute | solution.py:28
  78.8 1.9 collective-permute-start.10
  80.7 7.4 %collective-permute-start.11 = (f32[8,16,1,130]{3,1,2,0:T(8,128)S(1)}, f32[8,16,1,130]{3,1,2,0:T(8,128)S(1)}, u32[]{:S(2)}, u32[]{:S(2)}) collective-permute-start(f32[8,16,1,130]{3,1,2,0:T(8,128)S(1)} %get-tuple-element.665), channel_id=1, source_target_pairs={{1,0},{2,1},{3,2},{4,3},{5,4},{6,5},{7,6},{8,7},{9,8},{10,9},{11,1... | collective-permute-start | bytes 199688 | tf_op jit(solution)/shard_map/ppermute | solution.py:46
  89.2 1.3 collective-permute-done.11
  97.5 1.3 collective-permute-start.12
  98.8 3.0 %collective-permute-start.13 = (f32[8,16,2,1]{3,1,2,0:T(8,128)S(1)}, f32[8,16,2,1]{3,1,2,0:T(8,128)S(1)}, u32[]{:S(2)}, u32[]{:S(2)}) collective-permute-start(f32[8,16,2,1]{3,1,2,0:T(8,128)S(1)} %get-tuple-element.695), channel_id=1, source_target_pairs={{16,0},{32,16},{48,32},{64,48},{80,64},{96,80},{112,96},{128,112},... | collective-permute-start | bytes 3080 | tf_op jit(solution)/shard_map/ppermute | solution.py:30
  101.8 2.8 %collective-permute-done.12 = f32[8,16,2,1]{3,1,2,0:T(8,128)S(1)} collective-permute-done((f32[8,16,2,1]{3,1,2,0:T(8,128)S(1)}, f32[8,16,2,1]{3,1,2,0:T(8,128)S(1)}, u32[]{:S(2)}, u32[]{:S(2)}) %collective-permute-start.12) | collective-permute-done | bytes 1056 | tf_op jit(solution)/shard_map/ppermute | solution.py:28
  105.0 1.9 collective-permute-start.14
  107.0 7.9 %collective-permute-done.14 = f32[8,16,1,130]{3,1,2,0:T(8,128)S(1)} collective-permute-done((f32[8,16,1,130]{3,1,2,0:T(8,128)S(1)}, f32[8,16,1,130]{3,1,2,0:T(8,128)S(1)}, u32[]{:S(2)}, u32[]{:S(2)}) %collective-permute-start.14) | collective-permute-done | bytes 66592 | tf_op jit(solution)/shard_map/ppermute | solution.py:45
  114.9 1.9 collective-permute-start.15
  117.1 2.3 %collective-permute-done.15 = f32[8,16,1,130]{3,1,2,0:T(8,128)S(1)} collective-permute-done((f32[8,16,1,130]{3,1,2,0:T(8,128)S(1)}, f32[8,16,1,130]{3,1,2,0:T(8,128)S(1)}, u32[]{:S(2)}, u32[]{:S(2)}) %collective-permute-start.15) | collective-permute-done | bytes 66592 | tf_op jit(solution)/shard_map/ppermute | solution.py:46
  124.7 1.9 collective-permute-start.18
  126.7 3.7 %collective-permute-start.17 = (f32[8,16,2,1]{3,1,2,0:T(8,128)}, f32[8,16,2,1]{3,1,2,0:T(8,128)}, u32[]{:S(2)}, u32[]{:S(2)}) collective-permute-start(f32[8,16,2,1]{3,1,2,0:T(8,128)} %get-tuple-element.598), channel_id=1, source_target_pairs={{16,0},{32,16},{48,32},{64,48},{80,64},{96,80},{112,96},{128,112},... | collective-permute-start | bytes 3080 | tf_op jit(solution)/shard_map/ppermute | solution.py:30
  130.4 7.7 %collective-permute-start.19 = (f32[8,16,1,128]{3,1,2,0:T(8,128)}, f32[8,16,1,128]{3,1,2,0:T(8,128)}, u32[]{:S(2)}, u32[]{:S(2)}) collective-permute-start(f32[8,16,1,128]{3,1,2,0:T(8,128)} %get-tuple-element.565), channel_id=1, source_target_pairs={{1,0},{2,1},{3,2},{4,3},{5,4},{6,5},{7,6},{8,7},{9,8},{10,9},{11,1... | collective-permute-start | bytes 196616 | tf_op jit(solution)/shard_map/ppermute | solution.py:30
  138.9 1.0 scatter-add.144
  139.8 1.7 slice_add_fusion.19
  141.5 2.1 scatter-add.145
  149.8 1.1 multiply_reduce_fusion.9
  157.2 1.9 collective-permute-start.22
  159.2 4.2 %collective-permute-start.21 = (f32[8,16,2,1]{3,1,2,0:T(8,128)S(1)}, f32[8,16,2,1]{3,1,2,0:T(8,128)S(1)}, u32[]{:S(2)}, u32[]{:S(2)}) collective-permute-start(f32[8,16,2,1]{3,1,2,0:T(8,128)S(1)} %get-tuple-element.592), channel_id=1, source_target_pairs={{16,0},{32,16},{48,32},{64,48},{80,64},{96,80},{112,96},{128,112},... | collective-permute-start | bytes 3080 | tf_op jit(solution)/shard_map/ppermute | solution.py:30
  163.4 7.6 %collective-permute-start.23 = (f32[8,16,1,128]{3,1,2,0:T(8,128)}, f32[8,16,1,128]{3,1,2,0:T(8,128)}, u32[]{:S(2)}, u32[]{:S(2)}) collective-permute-start(f32[8,16,1,128]{3,1,2,0:T(8,128)} %get-tuple-element.563), channel_id=1, source_target_pairs={{1,0},{2,1},{3,2},{4,3},{5,4},{6,5},{7,6},{8,7},{9,8},{10,9},{11,1... | collective-permute-start | bytes 196616 | tf_op jit(solution)/shard_map/ppermute | solution.py:30
  171.3 1.2 scatter-add.151
  178.8 1.1 multiply_reduce_fusion.8
  186.0 1.9 collective-permute-start.26
  188.0 4.2 %collective-permute-start.25 = (f32[8,16,2,1]{3,1,2,0:T(8,128)S(1)}, f32[8,16,2,1]{3,1,2,0:T(8,128)S(1)}, u32[]{:S(2)}, u32[]{:S(2)}) collective-permute-start(f32[8,16,2,1]{3,1,2,0:T(8,128)S(1)} %get-tuple-element.586), channel_id=1, source_target_pairs={{16,0},{32,16},{48,32},{64,48},{80,64},{96,80},{112,96},{128,112},... | collective-permute-start | bytes 3080 | tf_op jit(solution)/shard_map/ppermute | solution.py:30
  192.2 7.6 %collective-permute-start.27 = (f32[8,16,1,128]{3,1,2,0:T(8,128)S(1)}, f32[8,16,1,128]{3,1,2,0:T(8,128)S(1)}, u32[]{:S(2)}, u32[]{:S(2)}) collective-permute-start(f32[8,16,1,128]{3,1,2,0:T(8,128)S(1)} %get-tuple-element.561), channel_id=1, source_target_pairs={{1,0},{2,1},{3,2},{4,3},{5,4},{6,5},{7,6},{8,7},{9,8},{10,9},{11,1... | collective-permute-start | bytes 196616 | tf_op jit(solution)/shard_map/ppermute | solution.py:30
  200.1 1.2 scatter-add.159
  205.3 1.1 multiply_reduce_fusion.7
  211.3 1.9 collective-permute-start.30
  213.2 4.2 %collective-permute-start.29 = (f32[8,16,2,1]{3,1,2,0:T(8,128)S(1)}, f32[8,16,2,1]{3,1,2,0:T(8,128)S(1)}, u32[]{:S(2)}, u32[]{:S(2)}) collective-permute-start(f32[8,16,2,1]{3,1,2,0:T(8,128)S(1)} %get-tuple-element.580), channel_id=1, source_target_pairs={{16,0},{32,16},{48,32},{64,48},{80,64},{96,80},{112,96},{128,112},... | collective-permute-start | bytes 3080 | tf_op jit(solution)/shard_map/ppermute | solution.py:30
  217.4 7.6 %collective-permute-start.31 = (f32[8,16,1,128]{3,1,2,0:T(8,128)S(1)}, f32[8,16,1,128]{3,1,2,0:T(8,128)S(1)}, u32[]{:S(2)}, u32[]{:S(2)}) collective-permute-start(f32[8,16,1,128]{3,1,2,0:T(8,128)S(1)} %get-tuple-element.559), channel_id=1, source_target_pairs={{1,0},{2,1},{3,2},{4,3},{5,4},{6,5},{7,6},{8,7},{9,8},{10,9},{11,1... | collective-permute-start | bytes 196616 | tf_op jit(solution)/shard_map/ppermute | solution.py:30
  226.0 1.2 scatter-add.165
  (513 shorter events, 67.9 us)
Async XLA Ops:
  3.1 7.6 %copy-start.7 = (f32[8,16,2,128]{3,2,1,0:T(2,128)S(1)}, f32[8,16,2,128]{3,2,1,0:T(2,128)}, u32[]{:S(2)}) copy-start(f32[8,16,2,128]{3,2,1,0:T(2,128)} %param.86) | copy-start | bytes 393220
  3.1 14.3 %all-to-all-start = ((f32[10,1,32,128]{3,0,1,2:T(8,128)}), f32[10,1,32,128]{3,0,1,2:T(8,128)S(1)}, u32[]{:S(2)}, u32[]{:S(2)}) async-start(f32[10,1,32,128]{3,0,1,2:T(8,128)} %copy.47), calls=%async_computation | async-start | bytes 524288 | tf_op jit(solution)/shard_map/all_to_all | solution.py:65
  17.6 7.1 %copy-start.70 = (f32[1,1,32,128]{3,0,1,2:T(1,128)}, f32[1,1,32,128]{3,0,1,2:T(1,128)S(1)}, u32[]{:S(2)}) copy-start(f32[1,1,32,128]{3,0,1,2:T(1,128)S(1)} %get-tuple-element.642) | copy-start | bytes 49156
  17.6 7.1 %copy-start.72 = (f32[1,1,32,128]{3,0,1,2:T(1,128)}, f32[1,1,32,128]{3,0,1,2:T(1,128)S(1)}, u32[]{:S(2)}) copy-start(f32[1,1,32,128]{3,0,1,2:T(1,128)S(1)} %get-tuple-element.643) | copy-start | bytes 49156
  17.7 78.9 %copy-start.15 = (f32[1,1,32,128]{3,0,1,2:T(1,128)}, f32[1,1,32,128]{3,0,1,2:T(1,128)S(1)}, u32[]{:S(2)}) copy-start(f32[1,1,32,128]{3,0,1,2:T(1,128)S(1)} %get-tuple-element.646) | copy-start | bytes 49156
  18.4 9.8 %collective-permute-start = (f32[8,16,2,1]{3,1,2,0:T(8,128)S(1)}, f32[8,16,2,1]{3,1,2,0:T(8,128)S(1)}, u32[]{:S(2)}, u32[]{:S(2)}) collective-permute-start(f32[8,16,2,1]{3,1,2,0:T(8,128)S(1)} %get-tuple-element.700), channel_id=1, source_target_pairs={{0,16},{16,32},{32,48},{48,64},{64,80},{80,96},{96,112},{112,128},... | collective-permute-start | bytes 3080 | tf_op jit(solution)/shard_map/ppermute | solution.py:28
  20.4 7.8 %collective-permute-start.1 = (f32[8,16,2,1]{3,1,2,0:T(8,128)S(1)}, f32[8,16,2,1]{3,1,2,0:T(8,128)S(1)}, u32[]{:S(2)}, u32[]{:S(2)}) collective-permute-start(f32[8,16,2,1]{3,1,2,0:T(8,128)S(1)} %get-tuple-element.701), channel_id=1, source_target_pairs={{16,0},{32,16},{48,32},{64,48},{80,64},{96,80},{112,96},{128,112},... | collective-permute-start | bytes 3080 | tf_op jit(solution)/shard_map/ppermute | solution.py:30
  25.4 71.8 %copy-start.91 = (f32[16,2,128]{2,0,1:T(8,128)}, f32[16,2,128]{2,0,1:T(8,128)S(1)}, u32[]{:S(2)}) copy-start(f32[16,2,128]{2,0,1:T(8,128)S(1)} %copy.50) | copy-start | bytes 49156
  28.5 9.2 %copy-start.58 = (f32[16,2,130]{2,0,1:T(8,128)}, f32[16,2,130]{2,0,1:T(8,128)S(1)}, u32[]{:S(2)}) copy-start(f32[16,2,130]{2,0,1:T(8,128)S(1)} %fusion.296) | copy-start | bytes 49924
  28.5 10.2 %collective-permute-start.2 = (f32[8,16,1,130]{3,1,2,0:T(8,128)S(1)}, f32[8,16,1,130]{3,1,2,0:T(8,128)S(1)}, u32[]{:S(2)}, u32[]{:S(2)}) collective-permute-start(f32[8,16,1,130]{3,1,2,0:T(8,128)S(1)} %get-tuple-element.672), channel_id=1, source_target_pairs={{0,1},{1,2},{2,3},{3,4},{4,5},{5,6},{6,7},{7,8},{8,9},{9,10},{10,1... | collective-permute-start | bytes 199688 | tf_op jit(solution)/shard_map/ppermute | solution.py:45
  30.4 9.8 %collective-permute-start.3 = (f32[8,16,1,130]{3,1,2,0:T(8,128)S(1)}, f32[8,16,1,130]{3,1,2,0:T(8,128)S(1)}, u32[]{:S(2)}, u32[]{:S(2)}) collective-permute-start(f32[8,16,1,130]{3,1,2,0:T(8,128)S(1)} %get-tuple-element.673), channel_id=1, source_target_pairs={{1,0},{2,1},{3,2},{4,3},{5,4},{6,5},{7,6},{8,7},{9,8},{10,9},{11,1... | collective-permute-start | bytes 199688 | tf_op jit(solution)/shard_map/ppermute | solution.py:46
  40.6 1.6 copy-start.4
  46.5 4.2 %copy-start.66 = (f32[1,16,2,128]{3,1,2,0:T(8,128)}, f32[1,16,2,128]{3,1,2,0:T(8,128)S(1)}, u32[]{:S(2)}) copy-start(f32[1,16,2,128]{3,1,2,0:T(8,128)S(1)} %get-tuple-element.515) | copy-start | bytes 49156
  46.5 7.1 %collective-permute-start.4 = (f32[8,16,2,1]{3,1,2,0:T(8,128)S(1)}, f32[8,16,2,1]{3,1,2,0:T(8,128)S(1)}, u32[]{:S(2)}, u32[]{:S(2)}) collective-permute-start(f32[8,16,2,1]{3,1,2,0:T(8,128)S(1)} %get-tuple-element.698), channel_id=1, source_target_pairs={{0,16},{16,32},{32,48},{48,64},{64,80},{80,96},{96,112},{112,128},... | collective-permute-start | bytes 3080 | tf_op jit(solution)/shard_map/ppermute | solution.py:28
  46.5 7.1 %collective-permute-start.5 = (f32[8,16,2,1]{3,1,2,0:T(8,128)S(1)}, f32[8,16,2,1]{3,1,2,0:T(8,128)S(1)}, u32[]{:S(2)}, u32[]{:S(2)}) collective-permute-start(f32[8,16,2,1]{3,1,2,0:T(8,128)S(1)} %get-tuple-element.699), channel_id=1, source_target_pairs={{16,0},{32,16},{48,32},{64,48},{80,64},{96,80},{112,96},{128,112},... | collective-permute-start | bytes 3080 | tf_op jit(solution)/shard_map/ppermute | solution.py:30
  53.8 9.2 %copy-start.60 = (f32[16,2,130]{2,0,1:T(8,128)}, f32[16,2,130]{2,0,1:T(8,128)S(1)}, u32[]{:S(2)}) copy-start(f32[16,2,130]{2,0,1:T(8,128)S(1)} %fusion.297) | copy-start | bytes 49924
  53.9 10.2 %collective-permute-start.6 = (f32[8,16,1,130]{3,1,2,0:T(8,128)S(1)}, f32[8,16,1,130]{3,1,2,0:T(8,128)S(1)}, u32[]{:S(2)}, u32[]{:S(2)}) collective-permute-start(f32[8,16,1,130]{3,1,2,0:T(8,128)S(1)} %get-tuple-element.668), channel_id=1, source_target_pairs={{0,1},{1,2},{2,3},{3,4},{4,5},{5,6},{6,7},{7,8},{8,9},{9,10},{10,1... | collective-permute-start | bytes 199688 | tf_op jit(solution)/shard_map/ppermute | solution.py:45
  55.8 9.8 %collective-permute-start.7 = (f32[8,16,1,130]{3,1,2,0:T(8,128)S(1)}, f32[8,16,1,130]{3,1,2,0:T(8,128)S(1)}, u32[]{:S(2)}, u32[]{:S(2)}) collective-permute-start(f32[8,16,1,130]{3,1,2,0:T(8,128)S(1)} %get-tuple-element.669), channel_id=1, source_target_pairs={{1,0},{2,1},{3,2},{4,3},{5,4},{6,5},{7,6},{8,7},{9,8},{10,9},{11,1... | collective-permute-start | bytes 199688 | tf_op jit(solution)/shard_map/ppermute | solution.py:46
  66.0 1.6 copy-start.5
  66.1 1.5 copy-start.19
  71.5 4.2 %copy-start.68 = (f32[1,16,2,128]{3,1,2,0:T(8,128)}, f32[1,16,2,128]{3,1,2,0:T(8,128)S(1)}, u32[]{:S(2)}) copy-start(f32[1,16,2,128]{3,1,2,0:T(8,128)S(1)} %get-tuple-element.494) | copy-start | bytes 49156
  71.5 7.1 %collective-permute-start.8 = (f32[8,16,2,1]{3,1,2,0:T(8,128)S(1)}, f32[8,16,2,1]{3,1,2,0:T(8,128)S(1)}, u32[]{:S(2)}, u32[]{:S(2)}) collective-permute-start(f32[8,16,2,1]{3,1,2,0:T(8,128)S(1)} %get-tuple-element.696), channel_id=1, source_target_pairs={{0,16},{16,32},{32,48},{48,64},{64,80},{80,96},{96,112},{112,128},... | collective-permute-start | bytes 3080 | tf_op jit(solution)/shard_map/ppermute | solution.py:28
  72.8 5.8 %collective-permute-start.9 = (f32[8,16,2,1]{3,1,2,0:T(8,128)S(1)}, f32[8,16,2,1]{3,1,2,0:T(8,128)S(1)}, u32[]{:S(2)}, u32[]{:S(2)}) collective-permute-start(f32[8,16,2,1]{3,1,2,0:T(8,128)S(1)} %get-tuple-element.697), channel_id=1, source_target_pairs={{16,0},{32,16},{48,32},{64,48},{80,64},{96,80},{112,96},{128,112},... | collective-permute-start | bytes 3080 | tf_op jit(solution)/shard_map/ppermute | solution.py:30
  75.6 3.1 %copy-start.64 = (f32[8,16,2,128]{3,1,2,0:T(8,128)}, f32[8,16,2,128]{3,1,2,0:T(8,128)S(1)}, u32[]{:S(2)}) copy-start(f32[8,16,2,128]{3,1,2,0:T(8,128)S(1)} %constant_dynamic-update-slice_fusion.10) | copy-start | bytes 393220
  78.8 9.4 %copy-start.62 = (f32[16,2,130]{2,0,1:T(8,128)}, f32[16,2,130]{2,0,1:T(8,128)S(1)}, u32[]{:S(2)}) copy-start(f32[16,2,130]{2,0,1:T(8,128)S(1)} %fusion.298) | copy-start | bytes 49924
  78.8 10.4 %collective-permute-start.10 = (f32[8,16,1,130]{3,1,2,0:T(8,128)S(1)}, f32[8,16,1,130]{3,1,2,0:T(8,128)S(1)}, u32[]{:S(2)}, u32[]{:S(2)}) collective-permute-start(f32[8,16,1,130]{3,1,2,0:T(8,128)S(1)} %get-tuple-element.664), channel_id=1, source_target_pairs={{0,1},{1,2},{2,3},{3,4},{4,5},{5,6},{6,7},{7,8},{8,9},{9,10},{10,1... | collective-permute-start | bytes 199688 | tf_op jit(solution)/shard_map/ppermute | solution.py:45
  80.7 9.8 %collective-permute-start.11 = (f32[8,16,1,130]{3,1,2,0:T(8,128)S(1)}, f32[8,16,1,130]{3,1,2,0:T(8,128)S(1)}, u32[]{:S(2)}, u32[]{:S(2)}) collective-permute-start(f32[8,16,1,130]{3,1,2,0:T(8,128)S(1)} %get-tuple-element.665), channel_id=1, source_target_pairs={{1,0},{2,1},{3,2},{4,3},{5,4},{6,5},{7,6},{8,7},{9,8},{10,9},{11,1... | collective-permute-start | bytes 199688 | tf_op jit(solution)/shard_map/ppermute | solution.py:46
  90.9 1.6 copy-start.6
  97.5 7.2 %collective-permute-start.12 = (f32[8,16,2,1]{3,1,2,0:T(8,128)S(1)}, f32[8,16,2,1]{3,1,2,0:T(8,128)S(1)}, u32[]{:S(2)}, u32[]{:S(2)}) collective-permute-start(f32[8,16,2,1]{3,1,2,0:T(8,128)S(1)} %get-tuple-element.694), channel_id=1, source_target_pairs={{0,16},{16,32},{32,48},{48,64},{64,80},{80,96},{96,112},{112,128},... | collective-permute-start | bytes 3080 | tf_op jit(solution)/shard_map/ppermute | solution.py:28
  98.8 5.9 %collective-permute-start.13 = (f32[8,16,2,1]{3,1,2,0:T(8,128)S(1)}, f32[8,16,2,1]{3,1,2,0:T(8,128)S(1)}, u32[]{:S(2)}, u32[]{:S(2)}) collective-permute-start(f32[8,16,2,1]{3,1,2,0:T(8,128)S(1)} %get-tuple-element.695), channel_id=1, source_target_pairs={{16,0},{32,16},{48,32},{64,48},{80,64},{96,80},{112,96},{128,112},... | collective-permute-start | bytes 3080 | tf_op jit(solution)/shard_map/ppermute | solution.py:30
  105.0 9.9 %collective-permute-start.14 = (f32[8,16,1,130]{3,1,2,0:T(8,128)S(1)}, f32[8,16,1,130]{3,1,2,0:T(8,128)S(1)}, u32[]{:S(2)}, u32[]{:S(2)}) collective-permute-start(f32[8,16,1,130]{3,1,2,0:T(8,128)S(1)} %slice.2212), channel_id=1, source_target_pairs={{0,1},{1,2},{2,3},{3,4},{4,5},{5,6},{6,7},{7,8},{8,9},{9,10},{10,1... | collective-permute-start | bytes 199688 | tf_op jit(solution)/shard_map/ppermute | solution.py:45
  114.9 4.4 %collective-permute-start.15 = (f32[8,16,1,130]{3,1,2,0:T(8,128)S(1)}, f32[8,16,1,130]{3,1,2,0:T(8,128)S(1)}, u32[]{:S(2)}, u32[]{:S(2)}) collective-permute-start(f32[8,16,1,130]{3,1,2,0:T(8,128)S(1)} %get-tuple-element.661), channel_id=1, source_target_pairs={{1,0},{2,1},{3,2},{4,3},{5,4},{6,5},{7,6},{8,7},{9,8},{10,9},{11,1... | collective-permute-start | bytes 199688 | tf_op jit(solution)/shard_map/ppermute | solution.py:46
  123.3 14.8 %collective-permute-start.16 = (f32[8,16,2,1]{3,1,2,0:T(8,128)S(1)}, f32[8,16,2,1]{3,1,2,0:T(8,128)S(1)}, u32[]{:S(2)}, u32[]{:S(2)}) collective-permute-start(f32[8,16,2,1]{3,1,2,0:T(8,128)S(1)} %get-tuple-element.599), channel_id=1, source_target_pairs={{0,16},{16,32},{32,48},{48,64},{64,80},{80,96},{96,112},{112,128},... | collective-permute-start | bytes 3080 | tf_op jit(solution)/shard_map/ppermute | solution.py:28
  124.7 18.9 %collective-permute-start.18 = (f32[8,16,1,128]{3,1,2,0:T(8,128)}, f32[8,16,1,128]{3,1,2,0:T(8,128)}, u32[]{:S(2)}, u32[]{:S(2)}) collective-permute-start(f32[8,16,1,128]{3,1,2,0:T(8,128)} %get-tuple-element.566), channel_id=1, source_target_pairs={{0,1},{1,2},{2,3},{3,4},{4,5},{5,6},{6,7},{7,8},{8,9},{9,10},{10,1... | collective-permute-start | bytes 196616 | tf_op jit(solution)/shard_map/ppermute | solution.py:28
  126.7 13.2 %collective-permute-start.17 = (f32[8,16,2,1]{3,1,2,0:T(8,128)}, f32[8,16,2,1]{3,1,2,0:T(8,128)}, u32[]{:S(2)}, u32[]{:S(2)}) collective-permute-start(f32[8,16,2,1]{3,1,2,0:T(8,128)} %get-tuple-element.598), channel_id=1, source_target_pairs={{16,0},{32,16},{48,32},{64,48},{80,64},{96,80},{112,96},{128,112},... | collective-permute-start | bytes 3080 | tf_op jit(solution)/shard_map/ppermute | solution.py:30
  130.4 14.1 %collective-permute-start.19 = (f32[8,16,1,128]{3,1,2,0:T(8,128)}, f32[8,16,1,128]{3,1,2,0:T(8,128)}, u32[]{:S(2)}, u32[]{:S(2)}) collective-permute-start(f32[8,16,1,128]{3,1,2,0:T(8,128)} %get-tuple-element.565), channel_id=1, source_target_pairs={{1,0},{2,1},{3,2},{4,3},{5,4},{6,5},{7,6},{8,7},{9,8},{10,9},{11,1... | collective-permute-start | bytes 196616 | tf_op jit(solution)/shard_map/ppermute | solution.py:30
  156.1 14.9 %collective-permute-start.20 = (f32[8,16,2,1]{3,1,2,0:T(8,128)S(1)}, f32[8,16,2,1]{3,1,2,0:T(8,128)S(1)}, u32[]{:S(2)}, u32[]{:S(2)}) collective-permute-start(f32[8,16,2,1]{3,1,2,0:T(8,128)S(1)} %get-tuple-element.593), channel_id=1, source_target_pairs={{0,16},{16,32},{32,48},{48,64},{64,80},{80,96},{96,112},{112,128},... | collective-permute-start | bytes 3080 | tf_op jit(solution)/shard_map/ppermute | solution.py:28
  157.2 15.3 %collective-permute-start.22 = (f32[8,16,1,128]{3,1,2,0:T(8,128)}, f32[8,16,1,128]{3,1,2,0:T(8,128)}, u32[]{:S(2)}, u32[]{:S(2)}) collective-permute-start(f32[8,16,1,128]{3,1,2,0:T(8,128)} %get-tuple-element.564), channel_id=1, source_target_pairs={{0,1},{1,2},{2,3},{3,4},{4,5},{5,6},{6,7},{7,8},{8,9},{9,10},{10,1... | collective-permute-start | bytes 196616 | tf_op jit(solution)/shard_map/ppermute | solution.py:28
  159.2 12.1 %collective-permute-start.21 = (f32[8,16,2,1]{3,1,2,0:T(8,128)S(1)}, f32[8,16,2,1]{3,1,2,0:T(8,128)S(1)}, u32[]{:S(2)}, u32[]{:S(2)}) collective-permute-start(f32[8,16,2,1]{3,1,2,0:T(8,128)S(1)} %get-tuple-element.592), channel_id=1, source_target_pairs={{16,0},{32,16},{48,32},{64,48},{80,64},{96,80},{112,96},{128,112},... | collective-permute-start | bytes 3080 | tf_op jit(solution)/shard_map/ppermute | solution.py:30
  163.4 10.1 %collective-permute-start.23 = (f32[8,16,1,128]{3,1,2,0:T(8,128)}, f32[8,16,1,128]{3,1,2,0:T(8,128)}, u32[]{:S(2)}, u32[]{:S(2)}) collective-permute-start(f32[8,16,1,128]{3,1,2,0:T(8,128)} %get-tuple-element.563), channel_id=1, source_target_pairs={{1,0},{2,1},{3,2},{4,3},{5,4},{6,5},{7,6},{8,7},{9,8},{10,9},{11,1... | collective-permute-start | bytes 196616 | tf_op jit(solution)/shard_map/ppermute | solution.py:30
  185.1 14.6 %collective-permute-start.24 = (f32[8,16,2,1]{3,1,2,0:T(8,128)S(1)}, f32[8,16,2,1]{3,1,2,0:T(8,128)S(1)}, u32[]{:S(2)}, u32[]{:S(2)}) collective-permute-start(f32[8,16,2,1]{3,1,2,0:T(8,128)S(1)} %get-tuple-element.587), channel_id=1, source_target_pairs={{0,16},{16,32},{32,48},{48,64},{64,80},{80,96},{96,112},{112,128},... | collective-permute-start | bytes 3080 | tf_op jit(solution)/shard_map/ppermute | solution.py:28
  186.0 15.3 %collective-permute-start.26 = (f32[8,16,1,128]{3,1,2,0:T(8,128)}, f32[8,16,1,128]{3,1,2,0:T(8,128)S(1)}, u32[]{:S(2)}, u32[]{:S(2)}) collective-permute-start(f32[8,16,1,128]{3,1,2,0:T(8,128)} %get-tuple-element.562), channel_id=1, source_target_pairs={{0,1},{1,2},{2,3},{3,4},{4,5},{5,6},{6,7},{7,8},{8,9},{9,10},{10,1... | collective-permute-start | bytes 196616 | tf_op jit(solution)/shard_map/ppermute | solution.py:28
  188.0 12.1 %collective-permute-start.25 = (f32[8,16,2,1]{3,1,2,0:T(8,128)S(1)}, f32[8,16,2,1]{3,1,2,0:T(8,128)S(1)}, u32[]{:S(2)}, u32[]{:S(2)}) collective-permute-start(f32[8,16,2,1]{3,1,2,0:T(8,128)S(1)} %get-tuple-element.586), channel_id=1, source_target_pairs={{16,0},{32,16},{48,32},{64,48},{80,64},{96,80},{112,96},{128,112},... | collective-permute-start | bytes 3080 | tf_op jit(solution)/shard_map/ppermute | solution.py:30
  192.2 9.5 %collective-permute-start.27 = (f32[8,16,1,128]{3,1,2,0:T(8,128)S(1)}, f32[8,16,1,128]{3,1,2,0:T(8,128)S(1)}, u32[]{:S(2)}, u32[]{:S(2)}) collective-permute-start(f32[8,16,1,128]{3,1,2,0:T(8,128)S(1)} %get-tuple-element.561), channel_id=1, source_target_pairs={{1,0},{2,1},{3,2},{4,3},{5,4},{6,5},{7,6},{8,7},{9,8},{10,9},{11,1... | collective-permute-start | bytes 196616 | tf_op jit(solution)/shard_map/ppermute | solution.py:30
  211.0 14.6 %collective-permute-start.28 = (f32[8,16,2,1]{3,1,2,0:T(8,128)S(1)}, f32[8,16,2,1]{3,1,2,0:T(8,128)S(1)}, u32[]{:S(2)}, u32[]{:S(2)}) collective-permute-start(f32[8,16,2,1]{3,1,2,0:T(8,128)S(1)} %get-tuple-element.581), channel_id=1, source_target_pairs={{0,16},{16,32},{32,48},{48,64},{64,80},{80,96},{96,112},{112,128},... | collective-permute-start | bytes 3080 | tf_op jit(solution)/shard_map/ppermute | solution.py:28
  211.3 15.9 %collective-permute-start.30 = (f32[8,16,1,128]{3,1,2,0:T(8,128)S(1)}, f32[8,16,1,128]{3,1,2,0:T(8,128)S(1)}, u32[]{:S(2)}, u32[]{:S(2)}) collective-permute-start(f32[8,16,1,128]{3,1,2,0:T(8,128)S(1)} %get-tuple-element.560), channel_id=1, source_target_pairs={{0,1},{1,2},{2,3},{3,4},{4,5},{5,6},{6,7},{7,8},{8,9},{9,10},{10,1... | collective-permute-start | bytes 196616 | tf_op jit(solution)/shard_map/ppermute | solution.py:28
  213.2 12.7 %collective-permute-start.29 = (f32[8,16,2,1]{3,1,2,0:T(8,128)S(1)}, f32[8,16,2,1]{3,1,2,0:T(8,128)S(1)}, u32[]{:S(2)}, u32[]{:S(2)}) collective-permute-start(f32[8,16,2,1]{3,1,2,0:T(8,128)S(1)} %get-tuple-element.580), channel_id=1, source_target_pairs={{16,0},{32,16},{48,32},{64,48},{80,64},{96,80},{112,96},{128,112},... | collective-permute-start | bytes 3080 | tf_op jit(solution)/shard_map/ppermute | solution.py:30
  217.4 9.9 %collective-permute-start.31 = (f32[8,16,1,128]{3,1,2,0:T(8,128)S(1)}, f32[8,16,1,128]{3,1,2,0:T(8,128)S(1)}, u32[]{:S(2)}, u32[]{:S(2)}) collective-permute-start(f32[8,16,1,128]{3,1,2,0:T(8,128)S(1)} %get-tuple-element.559), channel_id=1, source_target_pairs={{1,0},{2,1},{3,2},{4,3},{5,4},{6,5},{7,6},{8,7},{9,8},{10,9},{11,1... | collective-permute-start | bytes 196616 | tf_op jit(solution)/shard_map/ppermute | solution.py:30
  (107 other events, 84.7 us)
where the time goes:
time: 232 us; the launch traced here: 228 us
  starting transfers between devices  113 us (49%)
  local copies, waits for them, and re-layouts  42.1 us (18%)
  other arithmetic  37.1 us (16%)
  waiting for transfers between devices  32.2 us (14%)
  between operations  3.13 us (1%)
    ppermute x12, starting transfers between devices, extended(): lax.ppermute(head, axis, [((i + 1) % count, i) for i in range(ends)])  61 us
    unnamed x249, local copies, waits for them, and re-layouts  31.4 us
    ppermute x4, starting transfers between devices, padded_2(): lax.ppermute(first, axis, [(b, a) for a, b in up])  23.9 us
    ppermute x12, starting transfers between devices, extended(): lax.ppermute(tail, axis, [(i, (i + 1) % count) for i in range(ends)])  13.3 us
    ppermute x12, waiting for transfers between devices, extended(): lax.ppermute(tail, axis, [(i, (i + 1) % count) for i in range(ends)])  10.9 us
    ppermute x4, waiting for transfers between devices, padded_2(): lax.ppermute(last, axis, up)  7.94 us
    ppermute x4, starting transfers between devices, padded_2(): lax.ppermute(last, axis, up)  7.68 us
    all_to_all x1, starting transfers between devices, side_by_side(): lax.all_to_all(both, axis, split_axis=split_dim, concat_axis=concat_dim,...  7.58 us
  transfers between devices with their start and end apart: 33, of which 11 were waited for; matrix products, arithmetic and copies ran while one was open for 8% of the time, Pallas kernels for 0%

commit v1 on v0

v1 whole, which is shorter than its diff:
```python
import jax
import jax.numpy as jnp
from jax import lax
from jax.experimental import pallas as pl
from jax.experimental.pallas import tpu as pltpu
from jax.sharding import PartitionSpec as P

GAMMA1 = 0.3
DT = 0.06
E0 = 1.0 / 0.3 + 0.32

R = 4
NROW = 2 + 2 * R
NF = 10
BLK = 104
SLOTS, STRIDE, HALO = 4, 36, 6
CR = ("cross", "role")
F32 = jnp.float32


def iota_lane():
    return lax.broadcasted_iota(jnp.int32, (1, 8, 128), 2)


def rl(x, shift):
    shift %= 128
    return x if shift == 0 else pltpu.roll(x, shift, axis=x.ndim - 1)


def lane_p(x):
    return pltpu.roll(x, 127, axis=2)


def lane_m(x):
    return pltpu.roll(x, 1, axis=2)


def axial_p(x, sub):
    r = pltpu.roll(x, 7, axis=1)
    return jnp.where(sub == 7, jnp.concatenate([r[1:], x[1:]], axis=0), r)


def axial_m(x, sub):
    r = pltpu.roll(x, 1, axis=1)
    return jnp.where(sub == 0, jnp.concatenate([x[:1], r[:1]], axis=0), r)


def primitives(q, rate):
    r = 1.0 / q[0]
    u = [q[1] * r, q[2] * r, q[3] * r]
    kin = 0.5 * (q[1] * u[0] + q[2] * u[1] + q[3] * u[2])
    p = GAMMA1 * (q[4] - kin)
    inv_t = q[0] / p
    e1 = DT * jnp.exp(rate - inv_t)
    e2 = (2.0 * DT) * jnp.exp(-1.5 * inv_t)
    return r, u, p, inv_t, e1, e2


def relax(kind):
    return jnp.where(kind == 1.0, 2.0 * DT, 0.0), jnp.where(kind == 2.0, DT, 0.0)


def forward_row(q, rate, kind, sub):
    r, u, p, inv_t, e1, e2 = primitives(q, rate)
    ri, rs = relax(kind)
    w1 = e1 * q[5]
    w2 = e2 * q[6]
    hp = (0.5 * DT) * p
    ce = (1.0 - 12.0 * DT) - ri
    cm = ce - rs
    acc = [q[k] * (cm if k in (1, 2, 3) else ce) for k in range(8)]
    acc[0] = acc[0] + ri
    acc[1] = acc[1] + 0.8 * ri
    acc[4] = acc[4] + E0 * ri + (3.0 * w1 + 2.0 * w2)
    acc[5] = acc[5] + ri - w1
    acc[6] = acc[6] + (w1 - w2)
    acc[7] = acc[7] + w2
    radial = None
    for d in range(3):
        h = (0.5 * DT) * u[d]
        ha = h - 2.0 * DT
        hb = h + 2.0 * DT
        a = [q[k] * ha for k in range(8)]
        b = [q[k] * hb for k in range(8)]
        pu = hp * u[d]
        a[d + 1] = a[d + 1] + hp
        b[d + 1] = b[d + 1] + hp
        a[4] = a[4] + pu
        b[4] = b[4] + pu
        if d == 1:
            radial = (a, b)
        elif d == 0:
            acc = [acc[k] - axial_p(a[k], sub) + axial_m(b[k], sub) for k in range(8)]
        else:
            acc = [acc[k] - lane_p(a[k]) + lane_m(b[k]) for k in range(8)]
    return acc, radial[0], radial[1]


def adjoint_row(q, rate, kind, c, cp, cm, bz, sub, bax):
    r, u, p, inv_t, e1, e2 = primitives(q, rate)
    ri, rs = relax(kind)
    al1 = 3.0 * c[4] - c[5] + c[6]
    al2 = 2.0 * c[4] - c[6] + c[7]
    g1 = e1 * al1
    g2 = e2 * al2
    rate_grad = g1 * q[5]
    gg = (rate_grad + 1.5 * (g2 * q[6])) * inv_t
    ce = (1.0 - 12.0 * DT) - ri
    cmo = ce - rs
    out = [c[k] * (cmo if k in (1, 2, 3) else ce) for k in range(8)]
    out[5] = out[5] + g1
    out[6] = out[6] + g2
    gp = gg * inv_t * r
    rho = -gg * r
    total = [None] * 8
    for d in range(3):
        if d == 0:
            hi = [axial_p(c[k], sub) for k in range(8)]
            lo = [axial_m(c[k], sub) for k in range(8)]
            w = [(hi[k] - lo[k]) + bax * c[k] for k in range(8)]
        elif d == 1:
            hi, lo = cp, cm
            w = [(hi[k] - lo[k]) + bz * c[k] for k in range(8)]
        else:
            hi = [lane_p(c[k]) for k in range(8)]
            lo = [lane_m(c[k]) for k in range(8)]
            w = [hi[k] - lo[k] for k in range(8)]
        total = [hi[k] + lo[k] if total[k] is None else total[k] + (hi[k] + lo[k]) for k in range(8)]
        h = (0.5 * DT) * u[d]
        s = q[0] * w[0]
        for k in range(1, 8):
            s = s + q[k] * w[k]
        s = ((0.5 * DT) * r) * (s + p * w[4])
        out = [out[k] + h * w[k] for k in range(8)]
        out[d + 1] = out[d + 1] + s
        rho = rho - s * u[d]
        gp = gp + ((0.5 * DT) * w[d + 1] + h * w[4])
    gp = GAMMA1 * gp
    rho = rho + (0.5 * gp) * (u[0] * u[0] + u[1] * u[1] + u[2] * u[2])
    out[0] = out[0] + rho
    for j in range(3):
        out[j + 1] = out[j + 1] - gp * u[j]
    out[4] = out[4] + gp
    return [out[k] + (2.0 * DT) * total[k] for k in range(8)], rate_grad


def sub_index():
    return lax.broadcasted_iota(jnp.int32, (1, 8, 128), 1)


def axial_mend():
    t = lax.broadcasted_iota(jnp.int32, (2, 8, 128), 0)
    s = lax.broadcasted_iota(jnp.int32, (2, 8, 128), 1)
    return jnp.where((t == 1) & (s == 7), -2.0, jnp.where((t == 0) & (s == 0), 2.0, 0.0))


def radial_ends():
    pos = lax.axis_index("cross") * lax.axis_size("role") + lax.axis_index("role")
    count = lax.axis_size("cross") * lax.axis_size("role")
    first = R - 2 * pos
    last = R + 2 * (count - pos) - 1
    return first, last


def scalar_mend(j, first, last):
    return jnp.where(j == last, -2.0, jnp.where(j == first, 2.0, 0.0)).astype(F32)


def edge_rows(s):
    lane = iota_lane()
    pack = jnp.where(lane >= 2 * STRIDE, 2, jnp.where(lane >= STRIDE, 1, 0))
    return pack * SLOTS + s


def lane_between(a, b):
    lane = iota_lane()
    return (lane >= a) & (lane < b)


def build_kernel(x_ref, rate_ref, kind_ref, out_ref, pad_ref):
    n = out_ref.shape[0]
    rows = 2 * n
    for f in range(NF):
        v = x_ref[f, 0] if f < 8 else (rate_ref[0] if f == 8 else kind_ref[0].astype(F32))
        pad_ref[f, R : R + rows] = v
        pad_ref[f, 0:R] = jnp.broadcast_to(v[0:1], (R, 128))
        pad_ref[f, R + rows : 2 * R + rows] = jnp.broadcast_to(v[rows - 1 : rows], (R, 128))
    for d in range(n):
        for f in range(NF):
            out_ref[d, f * NROW : (f + 1) * NROW] = pad_ref[f, 2 * d : 2 * d + NROW]
        out_ref[d, NF * NROW :] = jnp.zeros((BLK - NF * NROW, 128), F32)


def spread_kernel(recv_ref, fa_ref, fal_ref, far_ref, s0_ref, f_ref, e_ref, fe_ref, left_ref, right_ref):
    def edges(v, j, fi, own, ri):
        p, s = j // SLOTS, j % SLOTS
        base = STRIDE * p
        a = rl(v, base + HALO)
        b = rl(v, base + 3 * HALO - (128 - 2 * HALO))
        m = lane_between(base + HALO, base + 3 * HALO)
        m2 = lane_between(base + HALO, base + 5 * HALO)
        w = jnp.where(m, a, b)
        own[s] = w if own[s] is None else jnp.where(m2, w, own[s])
        k = base + HALO * s
        mk = lane_between(k, k + HALO)
        to_left = rl(v, k)
        to_right = rl(v, k + HALO - 128)
        ri[0] = to_left if ri[0] is None else jnp.where(mk, to_left, ri[0])
        ri[1] = to_right if ri[1] is None else jnp.where(mk, to_right, ri[1])

    for f in range(NF):
        own, sends = [None] * SLOTS, [None, None]
        for j in range(NROW):
            v = recv_ref[pl.ds(f * NROW + j, 16, stride=BLK), :].reshape(2, 8, 128)
            s0_ref[f, j] = v
            edges(v, j, f, own, sends)
        for s in range(SLOTS):
            e_ref[f, s] = own[s]
        left_ref[f], right_ref[f] = sends[0], sends[1]
    for f in range(8):
        own, sends = [None] * SLOTS, [None, None]
        for i in range(6):
            src = (fal_ref, fa_ref, far_ref)[i // 2]
            v = src[pl.ds(f * 32 + i % 2, 16, stride=2), :].reshape(2, 8, 128)
            f_ref[f, i] = v
            edges(v, i + 2, f, own, sends)
        for s in range(SLOTS):
            fe_ref[f, s] = own[s]
        left_ref[NF + f], right_ref[NF + f] = sends[0], sends[1]


def load(ref, j):
    return [ref[k, j] for k in range(8)]


def store(ref, j, v):
    for k in range(8):
        ref[k, j] = v[k]


def main_kernel(s0_ref, f_ref, c2_ref, s1_ref, kg_ref, st_ref, a_ref, b_ref, c3_ref):
    sub, bax = sub_index(), axial_mend()
    first, last = radial_ends()

    def level(src, dst, lo, hi, mix):
        def one(j, _):
            acc, a, b = forward_row(load(src, j), s0_ref[8, j], s0_ref[9, j], sub)
            store(a_ref, j, a)
            store(b_ref, j, b)
            store(dst, j, acc)
            return 0

        def two(j, _):
            jp = jnp.minimum(j + 1, jnp.maximum(last, j))
            jm = jnp.maximum(j - 1, jnp.minimum(first, j))
            jp = jnp.where(j == last, j, j + 1)
            jm = jnp.where(j == first, j, j - 1)
            for k in range(8):
                v = dst[k, j] - a_ref[k, jp] + b_ref[k, jm]
                if mix:
                    v = 0.5 * s0_ref[k, j] + 0.5 * v
                dst[k, j] = v
            return 0

        lax.fori_loop(lo - 1, hi + 2, one, 0)
        lax.fori_loop(lo, hi + 1, two, 0)

    st1, st2, st3 = st_ref.at[0], st_ref.at[1], st_ref.at[2]
    level(s0_ref, st1, 1, NROW - 2, False)
    level(st1, st2, 2, NROW - 3, True)
    level(st2, st3, 3, NROW - 4, False)

    def adj3(j, _):
        jp = jnp.where(j == last, j, j + 1) - 2
        jm = jnp.where(j == first, j, j - 1) - 2
        o, g = adjoint_row(
            load(st3, j), s0_ref[8, j], s0_ref[9, j], load(f_ref, j - 2), load(f_ref, jp), load(f_ref, jm),
            scalar_mend(j, first, last), sub, bax,
        )
        store(c3_ref, j - 3, [0.5 * v for v in o])
        a_ref[0, j] = 0.5 * g
        store(s1_ref, j - 3, load(st1, j))
        return 0

    lax.fori_loop(3, 7, adj3, 0)

    def adj2(j, _):
        jp = jnp.where(j == last, j, j + 1) - 3
        jm = jnp.where(j == first, j, j - 1) - 3
        o, g = adjoint_row(
            load(st2, j), s0_ref[8, j], s0_ref[9, j], load(c3_ref, j - 3), load(c3_ref, jp), load(c3_ref, jm),
            scalar_mend(j, first, last), sub, bax,
        )
        for k in range(8):
            c2_ref[k, j - 4] = 0.5 * f_ref[k, j - 2] + o[k]
        kg_ref[j - 4] = a_ref[0, j] + g
        return 0

    lax.fori_loop(4, 6, adj2, 0)


def wrap_slots(ref, k, s, v):
    ref[k, s + 1] = v
    if s == 0:
        ref[k, SLOTS + 1] = rl(v, -STRIDE)
    if s == SLOTS - 1:
        ref[k, 0] = rl(v, STRIDE)


def edge_mend(s, first, last):
    rows = edge_rows(s)
    return rows == first, rows == last


def edge_adjoint(state, e_ref, c_ref, s, first, last, sub, bax):
    mf, ml = edge_mend(s, first, last)
    c = load(c_ref, s + 1)
    cp = [jnp.where(ml, c[k], c_ref[k, s + 2]) for k in range(8)]
    cm = [jnp.where(mf, c[k], c_ref[k, s]) for k in range(8)]
    bz = jnp.where(ml, -2.0, jnp.where(mf, 2.0, 0.0))
    return adjoint_row(load(state, s), e_ref[8, s], e_ref[9, s], c, cp, cm, bz, sub, bax)


def edge_kernel(e_ref, fe_ref, fl_ref, fr_ref, c2_ref, c2s_ref, s1_ref, kg_ref, e0_ref, st_ref, a_ref, b_ref, c_ref, fx_ref):
    sub, bax = sub_index(), axial_mend()
    first, last = radial_ends()

    def halo(v, f, s):
        for p in range(3):
            base = STRIDE * p
            v = jnp.where(lane_between(base, base + HALO), rl(fl_ref[f], -HALO * s), v)
            v = jnp.where(lane_between(base + 5 * HALO, base + 6 * HALO), rl(fr_ref[f], HALO * (5 - s)), v)
        return v

    for f in range(NF):
        for s in range(SLOTS):
            e0_ref[f, s] = halo(e_ref[f, s], f, s)
    for f in range(8):
        for s in range(SLOTS):
            wrap_slots(fx_ref, f, s, halo(fe_ref[f, s], NF + f, s))

    def level(src, dst, mix):
        for s in range(SLOTS):
            acc, a, b = forward_row(load(src, s), e0_ref[8, s], e0_ref[9, s], sub)
            store(dst, s, acc)
            for k in range(8):
                wrap_slots(a_ref, k, s, a[k])
                wrap_slots(b_ref, k, s, b[k])
        for s in range(SLOTS):
            mf, ml = edge_mend(s, first, last)
            for k in range(8):
                ap = jnp.where(ml, a_ref[k, s + 1], a_ref[k, s + 2])
                bm = jnp.where(mf, b_ref[k, s + 1], b_ref[k, s])
                v = dst[k, s] - ap + bm
                if mix:
                    v = 0.5 * e0_ref[k, s] + 0.5 * v
                dst[k, s] = v

    st2, st3 = st_ref.at[0], st_ref.at[1]
    level(e0_ref, s1_ref, False)
    level(s1_ref, st2, True)
    level(st2, st3, False)
    g3 = []
    for s in range(SLOTS):
        o, g = edge_adjoint(st3, e0_ref, fx_ref, s, first, last, sub, bax)
        for k in range(8):
            wrap_slots(c_ref, k, s, 0.5 * o[k])
        g3.append(0.5 * g)
    second = lane_between(2 * STRIDE, 128)
    res = []
    for s in range(2):
        o, g = edge_adjoint(st2, e0_ref, c_ref, s, first, last, sub, bax)
        kg_ref[s] = g3[s] + g
        res.append([0.5 * fx_ref[k, s + 1] + o[k] for k in range(8)])
    for k in range(8):
        c2s_ref[k, 0] = c2_ref[k, 0]
        c2s_ref[k, 1] = c2_ref[k, 1]
        c2s_ref[k, 2] = jnp.where(second, rl(res[1][k], STRIDE), res[0][k])


def final_kernel(own_ref, lo_ref, hi_ref, s1_ref, s1e_ref, s0_ref, e0_ref, kg_ref, kge_ref, out_ref, rg_ref,
                 c2_ref, c1_ref, ce_ref, c1e_ref):
    sub, bax = sub_index(), axial_mend()
    first, last = radial_ends()
    for i, ref in enumerate((lo_ref, own_ref, hi_ref)):
        for k in range(8):
            c2_ref[k, 2 * i] = ref[k, 0]
            c2_ref[k, 2 * i + 1] = ref[k, 1]
    low = lane_between(0, STRIDE)
    for k in range(8):
        lo, own, hi = lo_ref[k, 2], own_ref[k, 2], hi_ref[k, 2]
        wrap_slots(ce_ref, k, 0, own)
        wrap_slots(ce_ref, k, 1, rl(own, -STRIDE))
        wrap_slots(ce_ref, k, 2, jnp.where(low, rl(lo, -STRIDE), hi))
        wrap_slots(ce_ref, k, 3, jnp.where(low, rl(lo, -2 * STRIDE), rl(hi, -STRIDE)))

    def adj1(j, _):
        jp = jnp.where(j == last, j, j + 1) - 2
        jm = jnp.where(j == first, j, j - 1) - 2
        o, g = adjoint_row(
            load(s1_ref, j - 3), s0_ref[8, j], s0_ref[9, j], load(c2_ref, j - 2), load(c2_ref, jp), load(c2_ref, jm),
            scalar_mend(j, first, last), sub, bax,
        )
        for k in range(8):
            c1_ref[k, j - 3] = 0.5 * o[k]
        c1_ref[8, j - 3] = 0.5 * g
        return 0

    lax.fori_loop(3, 7, adj1, 0)
    ge = []
    for s in range(SLOTS):
        o, g = edge_adjoint(s1e_ref, e0_ref, ce_ref, s, first, last, sub, bax)
        for k in range(8):
            wrap_slots(c1e_ref, k, s, 0.5 * o[k])
        ge.append(0.5 * g)

    head = lane_between(0, HALO)
    tail = lane_between(128 - HALO, 128)

    def merge(m, e):
        return jnp.where(head, rl(e, -(STRIDE + HALO)), jnp.where(tail, rl(e, 128 - HALO - (STRIDE + 4 * HALO)), m))

    for s in range(2):
        j = s + R
        jp = jnp.where(j == last, j, j + 1) - 3
        jm = jnp.where(j == first, j, j - 1) - 3
        o, g = adjoint_row(
            load(s0_ref, j), s0_ref[8, j], s0_ref[9, j], load(c1_ref, j - 3), load(c1_ref, jp), load(c1_ref, jm),
            scalar_mend(j, first, last), sub, bax,
        )
        oe, gedge = edge_adjoint(e0_ref, e0_ref, c1e_ref, s, first, last, sub, bax)
        for k in range(8):
            v = merge(0.5 * c2_ref[k, j - 2] + o[k], 0.5 * ce_ref[k, s + 1] + oe[k])
            out_ref[pl.ds(k * 32 + s, 16, stride=2), :] = v.reshape(16, 128)
        v = merge(kg_ref[s] + c1_ref[8, j - 3] + g, kge_ref[s] + ge[s] + gedge)
        rg_ref[pl.ds(s, 16, stride=2), :] = v.reshape(16, 128)


def call(kernel, outs, scratch, *args):
    return pl.pallas_call(
        kernel,
        out_shape=[jax.ShapeDtypeStruct(o, F32) for o in outs],
        in_specs=[pl.BlockSpec(memory_space=pltpu.VMEM)] * len(args),
        out_specs=[pl.BlockSpec(memory_space=pltpu.VMEM)] * len(outs),
        scratch_shapes=[pltpu.VMEM(s, F32) for s in scratch],
    )(*args)


T = (2, 8, 128)


def shifted(x, axis, step, ring):
    n = lax.axis_size(axis)
    pairs = [(i, (i + step) % n) for i in range(n) if ring or 0 <= i + step < n]
    return lax.ppermute(x, axis, pairs)


def shards(checkpoint, rate, kinds, final_adjoint):
    n = lax.axis_size(CR)
    fa = final_adjoint.reshape(256, 128)
    fal = shifted(fa, CR, 1, False)
    far = shifted(fa, CR, -1, False)
    (send,) = call(build_kernel, [(n, BLK, 128)], [(NF, 2 * n + 2 * R, 128)], checkpoint, rate, kinds)
    recv = lax.all_to_all(send, CR, split_axis=0, concat_axis=0, tiled=True)
    s0, f, e, fe, left, right = call(
        spread_kernel,
        [(NF, NROW) + T, (8, 6) + T, (NF, SLOTS) + T, (8, SLOTS) + T, (NF + 8,) + T, (NF + 8,) + T],
        [],
        recv.reshape(n * BLK, 128), fa, fal, far,
    )
    from_right = shifted(left, "azim", -1, True)
    from_left = shifted(right, "azim", 1, True)
    c2, s1, kg = call(
        main_kernel,
        [(8, 2) + T, (8, 4) + T, (2,) + T],
        [(3, 8, NROW) + T, (8, NROW) + T, (8, NROW) + T, (8, 4) + T],
        s0, f,
    )
    c2s, s1e, kge, e0 = call(
        edge_kernel,
        [(8, 3) + T, (8, SLOTS) + T, (2,) + T, (NF, SLOTS) + T],
        [(2, 8, SLOTS) + T] + [(8, SLOTS + 2) + T] * 4,
        e, fe, from_left, from_right, c2,
    )
    lo = shifted(c2s, CR, 1, False)
    hi = shifted(c2s, CR, -1, False)
    out, rg = call(
        final_kernel,
        [(256, 128), (32, 128)],
        [(8, 6) + T, (9, 4) + T, (8, SLOTS + 2) + T, (8, SLOTS + 2) + T],
        c2s, lo, hi, s1, s1e, s0, e0, kg, kge,
    )
    return out.reshape(8, 16, 2, 128), rg.reshape(16, 2, 128)


def solution(mesh):
    return jax.shard_map(
        shards,
        mesh=mesh,
        in_specs=(
            P(None, CR, None, "azim"),
            P(CR, None, "azim"),
            P(CR, None, "azim"),
            P(None, None, CR, "azim"),
        ),
        out_specs=(P(None, None, CR, "azim"), P(None, CR, "azim")),
        check_vma=False,
    )
```

time: 232 us -> 67.5 us (0.29); the launches traced: 228 us -> 67.1 us
  starting transfers between devices: 113 us -> 27.5 us
  local copies, waits for them, and re-layouts: 42.1 us -> 2.32 us
  other arithmetic: 37.1 us -> 0 us
  Pallas kernels: 0 us -> 19.5 us
  waiting for transfers between devices: 32.2 us -> 17 us
  between operations: 3.13 us -> 0.69 us
    ppermute x32 -> x6, starting transfers between devices: 106 us -> 19.9 us  [shifted(): return lax.ppermute(x, axis, pairs)]
    unnamed x249 -> x16, local copies, waits for them, and re-layouts: 31.4 us -> 2.32 us
    pallas_call x0 -> x5, Pallas kernels: none -> 19.5 us  [call(): pl.pallas_call(kernel, out_shape=[jax.ShapeDtypeStruct(o, F32) for o in o...]
    ppermute x32 -> x6, waiting for transfers between devices: 25.6 us -> 17 us  [shifted(): return lax.ppermute(x, axis, pairs)]
    scatter-add x26 -> x0, other arithmetic: 7.91 us -> none  [the longest x9 4.28 us: cell_flux(): carried = carried.at[which_axis].add(thermodynamic_stress)]
    scatter-add x8 -> x0, local copies, waits for them, and re-layouts: 7.24 us -> none  [the longest x4 5.8 us: return_ghosts(): interior = interior.at[..., -1].add(arrived[..., 3])]
    all_to_all x1, waiting for transfers between devices: 6.68 us -> 0.01 us  [shards(): recv = lax.all_to_all(send, CR, split_axis=0, concat_axis=0, tiled=True)]
    add_any x28 -> x0, other arithmetic: 5.09 us -> none  [the longest x8 2.98 us: local_update(): padded = jnp.pad(fixed, ((0, 0), (1, 1), (0, 0), (0, 0)), mode='edge')]
  transfers between devices with their start and end apart: 33 -> 7, of which waited for: 11 -> 4; matrix products, arithmetic and copies ran while one was open for 8% -> 0% of each run, Pallas kernels for 0% -> 8%
where the time goes in v1:
time: 67.5 us; the launch traced here: 67.1 us
  starting transfers between devices  27.5 us (41%)
  Pallas kernels  19.5 us (29%)
  waiting for transfers between devices  17 us (25%)
  local copies, waits for them, and re-layouts  2.32 us (3%)
  between operations  0.69 us (1%)
    ppermute x6, starting transfers between devices, shifted(): return lax.ppermute(x, axis, pairs)  19.9 us
    pallas_call x5, Pallas kernels, call(): pl.pallas_call(kernel, out_shape=[jax.ShapeDtypeStruct(o, F32) for o in o...  19.5 us
    ppermute x6, waiting for transfers between devices, shifted(): return lax.ppermute(x, axis, pairs)  17 us
    all_to_all x1, starting transfers between devices, shards(): recv = lax.all_to_all(send, CR, split_axis=0, concat_axis=0, tiled=True)  7.58 us
    unnamed x16, local copies, waits for them, and re-layouts  2.32 us
  transfers between devices with their start and end apart: 7, of which 4 were waited for; matrix products, arithmetic and copies ran while one was open for 0% of the time, Pallas kernels for 8%

profile of v1, /device:TPU:6, one launch (start us, length us, event | category | flops | bytes accessed | tf_op | source)
XLA Modules:
  0.0 67.1 jit_solution(1563707512863378716)
XLA Ops:
  0.6 1.9 %shard_map.59 = f32[16,104,128]{2,1,0:T(8,128)} custom-call(f32[8,1,32,128]{3,2,1,0:T(8,128)} %x_ref.1, f32[1,32,128]{2,1,0:T(8,128)} %rate_ref.1, s32[1,32,128]{2,1,0:T(8,128)} %kind_ref.1), custom_call_target="tpu_custom_call" | custom-call | tf_op jit(solution)/shard_map/pallas_call | solution.py:440
  2.6 0.0 copy-start.5
  2.6 7.6 %all-to-all-start = ((f32[16,104,128]{2,1,0:T(8,128)}), f32[16,104,128]{2,1,0:T(8,128)S(1)}, u32[]{:S(2)}, u32[]{:S(2)}) async-start(f32[16,104,128]{2,1,0:T(8,128)} %shard_map.59), calls=%async_computation | async-start | bytes 1703936 | tf_op jit(solution)/shard_map/all_to_all | solution.py:464
  10.2 0.0 copy-done.5
  10.2 4.3 %collective-permute-start.1 = (f32[256,128]{1,0:T(8,128)S(1)}, f32[256,128]{1,0:T(8,128)S(1)}, u32[]{:S(2)}, u32[]{:S(2)}) collective-permute-start(f32[256,128]{1,0:T(8,128)S(1)} %bitcast.6), channel_id=1, source_target_pairs={{1,0},{2,1},{3,2},{4,3},{5,4},{6,5},{7,6},{8,7},{9,8},{10,9},{11,1... | collective-permute-start | bytes 393224 | tf_op jit(solution)/shard_map/ppermute | solution.py:455
  14.5 1.9 %collective-permute-start = (f32[256,128]{1,0:T(8,128)S(1)}, f32[256,128]{1,0:T(8,128)S(1)}, u32[]{:S(2)}, u32[]{:S(2)}) collective-permute-start(f32[256,128]{1,0:T(8,128)S(1)} %bitcast.7), channel_id=1, source_target_pairs={{0,1},{1,2},{2,3},{3,4},{4,5},{5,6},{6,7},{7,8},{8,9},{9,10},{10,1... | collective-permute-start | bytes 393224 | tf_op jit(solution)/shard_map/ppermute | solution.py:455
  16.4 5.0 %collective-permute-done.1.far_ref = f32[256,128]{1,0:T(8,128)S(1)} collective-permute-done((f32[256,128]{1,0:T(8,128)S(1)}, f32[256,128]{1,0:T(8,128)S(1)}, u32[]{:S(2)}, u32[]{:S(2)}) %collective-permute-start.1) | collective-permute-done | bytes 131104 | tf_op jit(solution)/shard_map/ppermute | solution.py:455
  21.4 0.0 copy-start.6
  21.4 3.1 %collective-permute-done.fal_ref = f32[256,128]{1,0:T(8,128)S(1)} collective-permute-done((f32[256,128]{1,0:T(8,128)S(1)}, f32[256,128]{1,0:T(8,128)S(1)}, u32[]{:S(2)}, u32[]{:S(2)}) %collective-permute-start) | collective-permute-done | bytes 131104 | tf_op jit(solution)/shard_map/ppermute | solution.py:455
  24.5 0.0 copy-start.7
  24.5 0.0 all-to-all-done
  24.5 0.0 copy-start
  24.5 0.0 copy-done.6
  24.5 0.6 copy-done.7
  25.2 0.3 copy-done
  25.5 3.3 %shard_map.60 = (f32[10,10,2,8,128]{4,3,2,1,0:T(8,128)}, f32[8,6,2,8,128]{4,3,2,1,0:T(8,128)}, f32[10,4,2,8,128]{4,3,2,1,0:T(8,128)}, f32[8,4,2,8,128]{4,3,2,1,0...) custom-call(f32[1664,128]{1,0:T(8,128)} %bitcast.4, f32[256,128]{1,0:T(8,128)} %bitcast.5, ...), custom_call_target="tpu_custom_call" | custom-call | tf_op jit(solution)/shard_map/pallas_call | solution.py:440
  28.8 1.9 %collective-permute-start.2 = (f32[18,2,8,128]{3,2,1,0:T(8,128)}, f32[18,2,8,128]{3,2,1,0:T(8,128)S(1)}, u32[]{:S(2)}, u32[]{:S(2)}) collective-permute-start(f32[18,2,8,128]{3,2,1,0:T(8,128)} %get-tuple-element.19), channel_id=1, source_target_pairs={{0,16},{16,32},{32,48},{48,64},{64,80},{80,96},{96,112},{112,128},... | collective-permute-start | bytes 442376 | tf_op jit(solution)/shard_map/ppermute | solution.py:455
  30.7 4.3 %collective-permute-start.3 = (f32[18,2,8,128]{3,2,1,0:T(8,128)}, f32[18,2,8,128]{3,2,1,0:T(8,128)S(1)}, u32[]{:S(2)}, u32[]{:S(2)}) collective-permute-start(f32[18,2,8,128]{3,2,1,0:T(8,128)} %get-tuple-element.20), channel_id=1, source_target_pairs={{0,240},{16,0},{32,16},{48,32},{64,48},{80,64},{96,80},{112,96},{1... | collective-permute-start | bytes 442376 | tf_op jit(solution)/shard_map/ppermute | solution.py:455
  35.0 5.7 %shard_map.61 = (f32[8,2,2,8,128]{4,3,2,1,0:T(8,128)}, f32[8,4,2,8,128]{4,3,2,1,0:T(8,128)}, f32[2,2,8,128]{3,2,1,0:T(8,128)}) custom-call(f32[10,10,2,8,128]{4,3,2,1,0:T(8,128)} %get-tuple-element.21.s0_ref, f32[8,6,2,8,128]{4,3,2,1,0:T(8,128)} %get-tuple-element.22.f_ref), custom_call_target="tpu_custom_call" | custom-call | tf_op jit(solution)/shard_map/pallas_call | solution.py:440
  40.7 0.0 collective-permute-done.2.fl_ref
  40.7 0.0 copy-start.3
  40.7 0.0 collective-permute-done.3.fr_ref
  40.7 0.0 copy-start.4
  40.7 0.6 copy-done.3
  41.4 0.1 copy-done.4
  41.4 4.6 %shard_map.62 = (f32[8,3,2,8,128]{4,3,2,1,0:T(8,128)}, f32[8,4,2,8,128]{4,3,2,1,0:T(8,128)}, f32[2,2,8,128]{3,2,1,0:T(8,128)}, f32[10,4,2,8,128]{4,3,2,1,0:T(8,128)}) custom-call(f32[10,4,2,8,128]{4,3,2,1,0:T(8,128)} %get-tuple-element.17.e_ref, f32[8,4,2,8,128]{4,3,2,1,0:T(8,128)} %get-tuple-element.18.fe_ref, f32[18,2,8,128]{3,2,1,0:T(8,128)} %copy-done.3, ...), custom_call_target="tpu_custom_call" | custom-call | tf_op jit(solution)/shard_map/pallas_call | solution.py:440
  46.0 5.6 %collective-permute-start.5 = (f32[8,3,2,8,128]{4,3,2,1,0:T(8,128)}, f32[8,3,2,8,128]{4,3,2,1,0:T(8,128)S(1)}, u32[]{:S(2)}, u32[]{:S(2)}) collective-permute-start(f32[8,3,2,8,128]{4,3,2,1,0:T(8,128)} %get-tuple-element.24.own_ref), channel_id=1, source_target_pairs={{1,0},{2,1},{3,2},{4,3},{5,4},{6,5},{7,6},{8,7},{9,8},{10,9},{11,1... | collective-permute-start | bytes 589832 | tf_op jit(solution)/shard_map/ppermute | solution.py:455
  51.6 1.9 %collective-permute-start.4 = (f32[8,3,2,8,128]{4,3,2,1,0:T(8,128)}, f32[8,3,2,8,128]{4,3,2,1,0:T(8,128)S(1)}, u32[]{:S(2)}, u32[]{:S(2)}) collective-permute-start(f32[8,3,2,8,128]{4,3,2,1,0:T(8,128)} %get-tuple-element.24.own_ref), channel_id=1, source_target_pairs={{0,1},{1,2},{2,3},{3,4},{4,5},{5,6},{6,7},{7,8},{8,9},{9,10},{10,1... | collective-permute-start | bytes 589832 | tf_op jit(solution)/shard_map/ppermute | solution.py:455
  53.6 1.6 %collective-permute-done.5.hi_ref = f32[8,3,2,8,128]{4,3,2,1,0:T(8,128)S(1)} collective-permute-done((f32[8,3,2,8,128]{4,3,2,1,0:T(8,128)}, f32[8,3,2,8,128]{4,3,2,1,0:T(8,128)S(1)}, u32[]{:S(2)}, u32[]{:S(2)}) %collective-permute-start.5) | collective-permute-done | bytes 196640 | tf_op jit(solution)/shard_map/ppermute | solution.py:455
  55.1 0.0 copy-start.1
  55.1 7.3 %collective-permute-done.4.lo_ref = f32[8,3,2,8,128]{4,3,2,1,0:T(8,128)S(1)} collective-permute-done((f32[8,3,2,8,128]{4,3,2,1,0:T(8,128)}, f32[8,3,2,8,128]{4,3,2,1,0:T(8,128)S(1)}, u32[]{:S(2)}, u32[]{:S(2)}) %collective-permute-start.4) | collective-permute-done | bytes 196640 | tf_op jit(solution)/shard_map/ppermute | solution.py:455
  62.5 0.0 copy-start.2
  62.5 0.0 copy-done.1
  62.5 0.7 copy-done.2
  63.1 4.0 %shard_map.63 = (f32[256,128]{1,0:T(8,128)}, f32[32,128]{1,0:T(8,128)}) custom-call(f32[8,3,2,8,128]{4,3,2,1,0:T(8,128)} %get-tuple-element.24.own_ref, f32[8,3,2,8,128]{4,3,2,1,0:T(8,128)} %copy-done.2, f32[8,3,2,8,128]{4,3,2,1,0:T(8,128)} %copy-done.1, f32[8,4,2,8,128]{4,3,2,1,0:T(8,128)} %get-tuple-element.25.s1_ref, ...), custom_call_target="tpu_custom_call" | custom-call | tf_op jit(solution)/shard_map/pallas_call | solution.py:440
Async XLA Ops:
  2.6 7.6 %copy-start.5 = (f32[8,16,2,128]{3,2,1,0:T(2,128)S(1)}, f32[8,16,2,128]{3,2,1,0:T(2,128)}, u32[]{:S(2)}) copy-start(f32[8,16,2,128]{3,2,1,0:T(2,128)} %param.7) | copy-start | bytes 393220
  2.6 22.0 %all-to-all-start = ((f32[16,104,128]{2,1,0:T(8,128)}), f32[16,104,128]{2,1,0:T(8,128)S(1)}, u32[]{:S(2)}, u32[]{:S(2)}) async-start(f32[16,104,128]{2,1,0:T(8,128)} %shard_map.59), calls=%async_computation | async-start | bytes 1703936 | tf_op jit(solution)/shard_map/all_to_all | solution.py:464
  10.2 11.2 %collective-permute-start.1 = (f32[256,128]{1,0:T(8,128)S(1)}, f32[256,128]{1,0:T(8,128)S(1)}, u32[]{:S(2)}, u32[]{:S(2)}) collective-permute-start(f32[256,128]{1,0:T(8,128)S(1)} %bitcast.6), channel_id=1, source_target_pairs={{1,0},{2,1},{3,2},{4,3},{5,4},{6,5},{7,6},{8,7},{9,8},{10,9},{11,1... | collective-permute-start | bytes 393224 | tf_op jit(solution)/shard_map/ppermute | solution.py:455
  14.5 10.1 %collective-permute-start = (f32[256,128]{1,0:T(8,128)S(1)}, f32[256,128]{1,0:T(8,128)S(1)}, u32[]{:S(2)}, u32[]{:S(2)}) collective-permute-start(f32[256,128]{1,0:T(8,128)S(1)} %bitcast.7), channel_id=1, source_target_pairs={{0,1},{1,2},{2,3},{3,4},{4,5},{5,6},{6,7},{7,8},{8,9},{9,10},{10,1... | collective-permute-start | bytes 393224 | tf_op jit(solution)/shard_map/ppermute | solution.py:455
  21.4 3.1 %copy-start.6 = (f32[256,128]{1,0:T(8,128)}, f32[256,128]{1,0:T(8,128)S(1)}, u32[]{:S(2)}) copy-start(f32[256,128]{1,0:T(8,128)S(1)} %collective-permute-done.1.far_ref) | copy-start | bytes 393220
  24.5 0.7 copy-start.7
  24.5 0.9 %copy-start = (f32[16,104,128]{2,1,0:T(8,128)}, f32[16,104,128]{2,1,0:T(8,128)S(1)}, u32[]{:S(2)}) copy-start(f32[16,104,128]{2,1,0:T(8,128)S(1)} %all-to-all-done) | copy-start | bytes 2555908
  28.8 11.9 %collective-permute-start.2 = (f32[18,2,8,128]{3,2,1,0:T(8,128)}, f32[18,2,8,128]{3,2,1,0:T(8,128)S(1)}, u32[]{:S(2)}, u32[]{:S(2)}) collective-permute-start(f32[18,2,8,128]{3,2,1,0:T(8,128)} %get-tuple-element.19), channel_id=1, source_target_pairs={{0,16},{16,32},{32,48},{48,64},{64,80},{80,96},{96,112},{112,128},... | collective-permute-start | bytes 442376 | tf_op jit(solution)/shard_map/ppermute | solution.py:455
  30.7 10.0 %collective-permute-start.3 = (f32[18,2,8,128]{3,2,1,0:T(8,128)}, f32[18,2,8,128]{3,2,1,0:T(8,128)S(1)}, u32[]{:S(2)}, u32[]{:S(2)}) collective-permute-start(f32[18,2,8,128]{3,2,1,0:T(8,128)} %get-tuple-element.20), channel_id=1, source_target_pairs={{0,240},{16,0},{32,16},{48,32},{64,48},{80,64},{96,80},{112,96},{1... | collective-permute-start | bytes 442376 | tf_op jit(solution)/shard_map/ppermute | solution.py:455
  40.7 0.7 copy-start.3
  40.7 0.7 %copy-start.4 = (f32[18,2,8,128]{3,2,1,0:T(8,128)}, f32[18,2,8,128]{3,2,1,0:T(8,128)S(1)}, u32[]{:S(2)}) copy-start(f32[18,2,8,128]{3,2,1,0:T(8,128)S(1)} %collective-permute-done.3.fr_ref) | copy-start | bytes 442372
  46.0 9.1 %collective-permute-start.5 = (f32[8,3,2,8,128]{4,3,2,1,0:T(8,128)}, f32[8,3,2,8,128]{4,3,2,1,0:T(8,128)S(1)}, u32[]{:S(2)}, u32[]{:S(2)}) collective-permute-start(f32[8,3,2,8,128]{4,3,2,1,0:T(8,128)} %get-tuple-element.24.own_ref), channel_id=1, source_target_pairs={{1,0},{2,1},{3,2},{4,3},{5,4},{6,5},{7,6},{8,7},{9,8},{10,9},{11,1... | collective-permute-start | bytes 589832 | tf_op jit(solution)/shard_map/ppermute | solution.py:455
  51.6 10.8 %collective-permute-start.4 = (f32[8,3,2,8,128]{4,3,2,1,0:T(8,128)}, f32[8,3,2,8,128]{4,3,2,1,0:T(8,128)S(1)}, u32[]{:S(2)}, u32[]{:S(2)}) collective-permute-start(f32[8,3,2,8,128]{4,3,2,1,0:T(8,128)} %get-tuple-element.24.own_ref), channel_id=1, source_target_pairs={{0,1},{1,2},{2,3},{3,4},{4,5},{5,6},{6,7},{7,8},{8,9},{9,10},{10,1... | collective-permute-start | bytes 589832 | tf_op jit(solution)/shard_map/ppermute | solution.py:455
  55.1 7.3 %copy-start.1 = (f32[8,3,2,8,128]{4,3,2,1,0:T(8,128)}, f32[8,3,2,8,128]{4,3,2,1,0:T(8,128)S(1)}, u32[]{:S(2)}) copy-start(f32[8,3,2,8,128]{4,3,2,1,0:T(8,128)S(1)} %collective-permute-done.5.hi_ref) | copy-start | bytes 589828
  62.5 0.7 %copy-start.2 = (f32[8,3,2,8,128]{4,3,2,1,0:T(8,128)}, f32[8,3,2,8,128]{4,3,2,1,0:T(8,128)S(1)}, u32[]{:S(2)}) copy-start(f32[8,3,2,8,128]{4,3,2,1,0:T(8,128)S(1)} %collective-permute-done.4.lo_ref) | copy-start | bytes 589828

commit v2 on v1

--- a/solution.py
+++ b/solution.py
@@ -436,31 +436,32 @@
         rg_ref[pl.ds(s, 16, stride=2), :] = v.reshape(16, 128)
 
 
-def call(kernel, outs, scratch, *args):
+def call(kernel, outs, scratch, *args, near=True, leave=False):
+    args = [pltpu.with_memory_space_constraint(a, pltpu.VMEM if near else pltpu.HBM) for a in args]
     return pl.pallas_call(
         kernel,
-        out_shape=[jax.ShapeDtypeStruct(o, F32) for o in outs],
+        out_shape=[jax.ShapeDtypeStruct(o, F32) if leave else pltpu.VMEM(o, F32) for o in outs],
         in_specs=[pl.BlockSpec(memory_space=pltpu.VMEM)] * len(args),
         out_specs=[pl.BlockSpec(memory_space=pltpu.VMEM)] * len(outs),
         scratch_shapes=[pltpu.VMEM(s, F32) for s in scratch],
+        compiler_params=pltpu.CompilerParams(vmem_limit_bytes=8 * 1024 * 1024),
     )(*args)
 
 
 T = (2, 8, 128)
 
 
-def shifted(x, axis, step, ring):
+def shifted(x, axis, step):
     n = lax.axis_size(axis)
-    pairs = [(i, (i + step) % n) for i in range(n) if ring or 0 <= i + step < n]
-    return lax.ppermute(x, axis, pairs)
+    return lax.ppermute(x, axis, [(i, (i + step) % n) for i in range(n)])
 
 
 def shards(checkpoint, rate, kinds, final_adjoint):
     n = lax.axis_size(CR)
     fa = final_adjoint.reshape(256, 128)
-    fal = shifted(fa, CR, 1, False)
-    far = shifted(fa, CR, -1, False)
-    (send,) = call(build_kernel, [(n, BLK, 128)], [(NF, 2 * n + 2 * R, 128)], checkpoint, rate, kinds)
+    fal = shifted(fa, CR, 1)
+    far = shifted(fa, CR, -1)
+    (send,) = call(build_kernel, [(n, BLK, 128)], [(NF, 2 * n + 2 * R, 128)], checkpoint, rate, kinds, near=False, leave=True)
     recv = lax.all_to_all(send, CR, split_axis=0, concat_axis=0, tiled=True)
     s0, f, e, fe, left, right = call(
         spread_kernel,
@@ -468,8 +469,8 @@
         [],
         recv.reshape(n * BLK, 128), fa, fal, far,
     )
-    from_right = shifted(left, "azim", -1, True)
-    from_left = shifted(right, "azim", 1, True)
+    from_right = shifted(left, "azim", -1)
+    from_left = shifted(right, "azim", 1)
     c2, s1, kg = call(
         main_kernel,
         [(8, 2) + T, (8, 4) + T, (2,) + T],
@@ -482,13 +483,13 @@
         [(2, 8, SLOTS) + T] + [(8, SLOTS + 2) + T] * 4,
         e, fe, from_left, from_right, c2,
     )
-    lo = shifted(c2s, CR, 1, False)
-    hi = shifted(c2s, CR, -1, False)
+    lo = shifted(c2s, CR, 1)
+    hi = shifted(c2s, CR, -1)
     out, rg = call(
         final_kernel,
         [(256, 128), (32, 128)],
         [(8, 6) + T, (9, 4) + T, (8, SLOTS + 2) + T, (8, SLOTS + 2) + T],
-        c2s, lo, hi, s1, s1e, s0, e0, kg, kge,
+        c2s, lo, hi, s1, s1e, s0, e0, kg, kge, leave=True,
     )
     return out.reshape(8, 16, 2, 128), rg.reshape(16, 2, 128)
 

time: 67.5 us -> 53.6 us (0.79)
  Pallas kernels: 19.5 us -> 12 us
  starting transfers between devices: 27.5 us -> 20.2 us
  waiting for transfers between devices: 17 us -> 20.6 us
  local copies, waits for them, and re-layouts: 2.32 us -> 0.01 us
    pallas_call x5, Pallas kernels: 19.5 us -> 12 us  [call(): pl.pallas_call(kernel, out_shape=[jax.ShapeDtypeStruct(o, F32) if leave e...]
    ppermute x6, starting transfers between devices: 19.9 us -> 12.6 us  [shifted(): return lax.ppermute(x, axis, [(i, (i + step) % n) for i in range(n)])]
    ppermute x6, waiting for transfers between devices: 17 us -> 20.6 us  [shifted(): return lax.ppermute(x, axis, [(i, (i + step) % n) for i in range(n)])]
    unnamed x16 -> x2, local copies, waits for them, and re-layouts: 2.32 us -> 0.01 us
  transfers between devices with their start and end apart: 7 -> 7, of which waited for: 4 -> 4; matrix products, arithmetic and copies ran while one was open for 0% -> 0% of each run, Pallas kernels for 8% -> 7%
where the time goes in v2:
time: 53.6 us; the launch traced here: 53.4 us
  waiting for transfers between devices  20.6 us (38%)
  starting transfers between devices  20.2 us (38%)
  Pallas kernels  12 us (22%)
  between operations  0.68 us (1%)
    ppermute x6, waiting for transfers between devices, shifted(): return lax.ppermute(x, axis, [(i, (i + step) % n) for i in range(n)])  20.6 us
    ppermute x6, starting transfers between devices, shifted(): return lax.ppermute(x, axis, [(i, (i + step) % n) for i in range(n)])  12.6 us
    pallas_call x5, Pallas kernels, call(): pl.pallas_call(kernel, out_shape=[jax.ShapeDtypeStruct(o, F32) if leave e...  12 us
    all_to_all x1, starting transfers between devices, shards(): recv = lax.all_to_all(send, CR, split_axis=0, concat_axis=0, tiled=True)  7.58 us
  transfers between devices with their start and end apart: 7, of which 4 were waited for; matrix products, arithmetic and copies ran while one was open for 0% of the time, Pallas kernels for 7%

profile of v2, /device:TPU:6, one launch (start us, length us, event | category | flops | bytes accessed | tf_op | source)
XLA Modules:
  0.0 53.4 jit_solution(2743194892691877933)
XLA Ops:
  0.6 2.0 %shard_map.59 = f32[16,104,128]{2,1,0:T(8,128)} custom-call(f32[8,1,32,128]{3,2,1,0:T(8,128)} %x_ref.1, f32[1,32,128]{2,1,0:T(8,128)} %rate_ref.1, s32[1,32,128]{2,1,0:T(8,128)} %kind_ref.1), custom_call_target="tpu_custom_call" | custom-call | tf_op jit(solution)/shard_map/pallas_call | solution.py:441
  2.6 0.0 copy-start
  2.6 7.6 %all-to-all-start = ((f32[16,104,128]{2,1,0:T(8,128)}), f32[16,104,128]{2,1,0:T(8,128)S(1)}, u32[]{:S(2)}, u32[]{:S(2)}) async-start(f32[16,104,128]{2,1,0:T(8,128)} %shard_map.59), calls=%async_computation | async-start | bytes 1703936 | tf_op jit(solution)/shard_map/all_to_all | solution.py:465
  10.2 0.0 copy-done
  10.2 2.5 %collective-permute-start.1 = (f32[256,128]{1,0:T(8,128)S(1)}, f32[256,128]{1,0:T(8,128)S(1)}, u32[]{:S(2)}, u32[]{:S(2)}) collective-permute-start(f32[256,128]{1,0:T(8,128)S(1)} %bitcast.5), channel_id=1, source_target_pairs={{0,15},{1,0},{2,1},{3,2},{4,3},{5,4},{6,5},{7,6},{8,7},{9,8},{10,9... | collective-permute-start | bytes 393224 | tf_op jit(solution)/shard_map/ppermute | solution.py:456
  12.6 0.0 collective-permute-start
  12.7 8.8 %collective-permute-done.1.far_ref = f32[256,128]{1,0:T(8,128)S(1)} collective-permute-done((f32[256,128]{1,0:T(8,128)S(1)}, f32[256,128]{1,0:T(8,128)S(1)}, u32[]{:S(2)}, u32[]{:S(2)}) %collective-permute-start.1) | collective-permute-done | bytes 131104 | tf_op jit(solution)/shard_map/ppermute | solution.py:456
  21.4 3.1 %collective-permute-done.fal_ref = f32[256,128]{1,0:T(8,128)S(1)} collective-permute-done((f32[256,128]{1,0:T(8,128)S(1)}, f32[256,128]{1,0:T(8,128)S(1)}, u32[]{:S(2)}, u32[]{:S(2)}) %collective-permute-start) | collective-permute-done | bytes 131104 | tf_op jit(solution)/shard_map/ppermute | solution.py:456
  24.5 0.0 all-to-all-done
  24.5 1.1 %shard_map.60 = (f32[10,10,2,8,128]{4,3,2,1,0:T(8,128)S(1)}, f32[8,6,2,8,128]{4,3,2,1,0:T(8,128)S(1)}, f32[10,4,2,8,128]{4,3,2,1,0:T(8,128)S(1)}, f32[8,4,2,8,12...) custom-call(f32[1664,128]{1,0:T(8,128)S(1)} %bitcast.4, f32[256,128]{1,0:T(8,128)S(1)} %bitcast.7, ...), custom_call_target="tpu_custom_call" | custom-call | tf_op jit(solution)/shard_map/pallas_call | solution.py:441
  25.7 2.0 %collective-permute-start.2 = (f32[18,2,8,128]{3,2,1,0:T(8,128)S(1)}, f32[18,2,8,128]{3,2,1,0:T(8,128)S(1)}, u32[]{:S(2)}, u32[]{:S(2)}) collective-permute-start(f32[18,2,8,128]{3,2,1,0:T(8,128)S(1)} %get-tuple-element.19), channel_id=1, source_target_pairs={{0,16},{16,32},{32,48},{48,64},{64,80},{80,96},{96,112},{112,128},... | collective-permute-start | bytes 442376 | tf_op jit(solution)/shard_map/ppermute | solution.py:456
  27.7 4.4 %collective-permute-start.3 = (f32[18,2,8,128]{3,2,1,0:T(8,128)S(1)}, f32[18,2,8,128]{3,2,1,0:T(8,128)S(1)}, u32[]{:S(2)}, u32[]{:S(2)}) collective-permute-start(f32[18,2,8,128]{3,2,1,0:T(8,128)S(1)} %get-tuple-element.20), channel_id=1, source_target_pairs={{0,240},{16,0},{32,16},{48,32},{64,48},{80,64},{96,80},{112,96},{1... | collective-permute-start | bytes 442376 | tf_op jit(solution)/shard_map/ppermute | solution.py:456
  32.0 3.8 %shard_map.61 = (f32[8,2,2,8,128]{4,3,2,1,0:T(8,128)S(1)}, f32[8,4,2,8,128]{4,3,2,1,0:T(8,128)S(1)}, f32[2,2,8,128]{3,2,1,0:T(8,128)S(1)}) custom-call(f32[10,10,2,8,128]{4,3,2,1,0:T(8,128)S(1)} %get-tuple-element.21.s0_ref, f32[8,6,2,8,128]{4,3,2,1,0:T(8,128)S(1)} %get-tuple-element.22.f_ref), custom_call_target="tpu_custom_call" | custom-call | tf_op jit(solution)/shard_map/pallas_call | solution.py:441
  35.9 0.0 collective-permute-done.2.fl_ref
  35.9 0.0 collective-permute-done.3.fr_ref
  35.9 2.7 %shard_map.62 = (f32[8,3,2,8,128]{4,3,2,1,0:T(8,128)S(1)}, f32[8,4,2,8,128]{4,3,2,1,0:T(8,128)S(1)}, f32[2,2,8,128]{3,2,1,0:T(8,128)S(1)}, f32[10,4,2,8,128]{4,3,2,1,0:T(8,128)S(1)}) custom-call(f32[10,4,2,8,128]{4,3,2,1,0:T(8,128)S(1)} %get-tuple-element.17.e_ref, f32[8,4,2,8,128]{4,3,2,1,0:T(8,128)S(1)} %get-tuple-element.18.fe_ref, ...), custom_call_target="tpu_custom_call" | custom-call | tf_op jit(solution)/shard_map/pallas_call | solution.py:441
  38.6 3.8 %collective-permute-start.5 = (f32[8,3,2,8,128]{4,3,2,1,0:T(8,128)S(1)}, f32[8,3,2,8,128]{4,3,2,1,0:T(8,128)S(1)}, u32[]{:S(2)}, u32[]{:S(2)}) collective-permute-start(f32[8,3,2,8,128]{4,3,2,1,0:T(8,128)S(1)} %get-tuple-element.24.own_ref), channel_id=1, source_target_pairs={{0,15},{1,0},{2,1},{3,2},{4,3},{5,4},{6,5},{7,6},{8,7},{9,8},{10,9... | collective-permute-start | bytes 589832 | tf_op jit(solution)/shard_map/ppermute | solution.py:456
  42.4 0.0 collective-permute-start.4
  42.4 3.2 %collective-permute-done.5.hi_ref = f32[8,3,2,8,128]{4,3,2,1,0:T(8,128)S(1)} collective-permute-done((f32[8,3,2,8,128]{4,3,2,1,0:T(8,128)S(1)}, f32[8,3,2,8,128]{4,3,2,1,0:T(8,128)S(1)}, u32[]{:S(2)}, u32[]{:S(2)}) %collective-permute-start.5) | collective-permute-done | bytes 196640 | tf_op jit(solution)/shard_map/ppermute | solution.py:456
  45.6 5.5 %collective-permute-done.4.lo_ref = f32[8,3,2,8,128]{4,3,2,1,0:T(8,128)S(1)} collective-permute-done((f32[8,3,2,8,128]{4,3,2,1,0:T(8,128)S(1)}, f32[8,3,2,8,128]{4,3,2,1,0:T(8,128)S(1)}, u32[]{:S(2)}, u32[]{:S(2)}) %collective-permute-start.4) | collective-permute-done | bytes 196640 | tf_op jit(solution)/shard_map/ppermute | solution.py:456
  51.1 2.3 %shard_map.63 = (f32[256,128]{1,0:T(8,128)}, f32[32,128]{1,0:T(8,128)}) custom-call(f32[8,3,2,8,128]{4,3,2,1,0:T(8,128)S(1)} %get-tuple-element.24.own_ref, f32[8,3,2,8,128]{4,3,2,1,0:T(8,128)S(1)} %collective-permute-done.4.lo_ref, f32[8,3,2,8,128]{4,3,2,1,0:T(8,128)S(1)} %collective-permute-done.5.hi_ref, ...), custom_call_target="tpu_custom_call" | custom-call | tf_op jit(solution)/shard_map/pallas_call | solution.py:441
Async XLA Ops:
  2.6 7.6 %copy-start = (f32[8,16,2,128]{3,2,1,0:T(2,128)S(1)}, f32[8,16,2,128]{3,2,1,0:T(2,128)}, u32[]{:S(2)}) copy-start(f32[8,16,2,128]{3,2,1,0:T(2,128)} %param.7) | copy-start | bytes 393220
  2.6 22.0 %all-to-all-start = ((f32[16,104,128]{2,1,0:T(8,128)}), f32[16,104,128]{2,1,0:T(8,128)S(1)}, u32[]{:S(2)}, u32[]{:S(2)}) async-start(f32[16,104,128]{2,1,0:T(8,128)} %shard_map.59), calls=%async_computation | async-start | bytes 1703936 | tf_op jit(solution)/shard_map/all_to_all | solution.py:465
  10.2 11.2 %collective-permute-start.1 = (f32[256,128]{1,0:T(8,128)S(1)}, f32[256,128]{1,0:T(8,128)S(1)}, u32[]{:S(2)}, u32[]{:S(2)}) collective-permute-start(f32[256,128]{1,0:T(8,128)S(1)} %bitcast.5), channel_id=1, source_target_pairs={{0,15},{1,0},{2,1},{3,2},{4,3},{5,4},{6,5},{7,6},{8,7},{9,8},{10,9... | collective-permute-start | bytes 393224 | tf_op jit(solution)/shard_map/ppermute | solution.py:456
  12.6 11.9 %collective-permute-start = (f32[256,128]{1,0:T(8,128)S(1)}, f32[256,128]{1,0:T(8,128)S(1)}, u32[]{:S(2)}, u32[]{:S(2)}) collective-permute-start(f32[256,128]{1,0:T(8,128)S(1)} %bitcast.6), channel_id=1, source_target_pairs={{0,1},{1,2},{2,3},{3,4},{4,5},{5,6},{6,7},{7,8},{8,9},{9,10},{10,1... | collective-permute-start | bytes 393224 | tf_op jit(solution)/shard_map/ppermute | solution.py:456
  25.7 10.2 %collective-permute-start.2 = (f32[18,2,8,128]{3,2,1,0:T(8,128)S(1)}, f32[18,2,8,128]{3,2,1,0:T(8,128)S(1)}, u32[]{:S(2)}, u32[]{:S(2)}) collective-permute-start(f32[18,2,8,128]{3,2,1,0:T(8,128)S(1)} %get-tuple-element.19), channel_id=1, source_target_pairs={{0,16},{16,32},{32,48},{48,64},{64,80},{80,96},{96,112},{112,128},... | collective-permute-start | bytes 442376 | tf_op jit(solution)/shard_map/ppermute | solution.py:456
  27.7 8.2 %collective-permute-start.3 = (f32[18,2,8,128]{3,2,1,0:T(8,128)S(1)}, f32[18,2,8,128]{3,2,1,0:T(8,128)S(1)}, u32[]{:S(2)}, u32[]{:S(2)}) collective-permute-start(f32[18,2,8,128]{3,2,1,0:T(8,128)S(1)} %get-tuple-element.20), channel_id=1, source_target_pairs={{0,240},{16,0},{32,16},{48,32},{64,48},{80,64},{96,80},{112,96},{1... | collective-permute-start | bytes 442376 | tf_op jit(solution)/shard_map/ppermute | solution.py:456
  38.6 6.9 %collective-permute-start.5 = (f32[8,3,2,8,128]{4,3,2,1,0:T(8,128)S(1)}, f32[8,3,2,8,128]{4,3,2,1,0:T(8,128)S(1)}, u32[]{:S(2)}, u32[]{:S(2)}) collective-permute-start(f32[8,3,2,8,128]{4,3,2,1,0:T(8,128)S(1)} %get-tuple-element.24.own_ref), channel_id=1, source_target_pairs={{0,15},{1,0},{2,1},{3,2},{4,3},{5,4},{6,5},{7,6},{8,7},{9,8},{10,9... | collective-permute-start | bytes 589832 | tf_op jit(solution)/shard_map/ppermute | solution.py:456
  42.4 8.7 %collective-permute-start.4 = (f32[8,3,2,8,128]{4,3,2,1,0:T(8,128)S(1)}, f32[8,3,2,8,128]{4,3,2,1,0:T(8,128)S(1)}, u32[]{:S(2)}, u32[]{:S(2)}) collective-permute-start(f32[8,3,2,8,128]{4,3,2,1,0:T(8,128)S(1)} %get-tuple-element.24.own_ref), channel_id=1, source_target_pairs={{0,1},{1,2},{2,3},{3,4},{4,5},{5,6},{6,7},{7,8},{8,9},{9,10},{10,1... | collective-permute-start | bytes 589832 | tf_op jit(solution)/shard_map/ppermute | solution.py:456

commit v3 on v2

v3 whole, which is shorter than its diff:
```python
import jax
import jax.numpy as jnp
from jax import lax
from jax.experimental import pallas as pl
from jax.experimental.pallas import tpu as pltpu
from jax.sharding import PartitionSpec as P


GAMMA1 = 0.3
DT = 0.06
E0 = 1.0 / 0.3 + 0.32

R = 6
RF = 4
NROW = 2 + 2 * R
NFA = 2 + 2 * RF
CHIP = NROW + 2
NF = 10
BLK = NF * CHIP
SLOTS, STRIDE, HALO = 5, 36, 6
CR = ("cross", "role")
F32 = jnp.float32


def iota_lane():
    return lax.broadcasted_iota(jnp.int32, (1, 8, 128), 2)


def rl(x, shift):
    shift %= 128
    return x if shift == 0 else pltpu.roll(x, shift, axis=x.ndim - 1)


def lane_p(x):
    return pltpu.roll(x, 127, axis=2)


def lane_m(x):
    return pltpu.roll(x, 1, axis=2)


def axial_p(x, sub):
    return jnp.concatenate([x[1:], jnp.where(sub == 7, x[1:], pltpu.roll(x[:1], 7, axis=1))], axis=0)


def axial_m(x, sub):
    return jnp.concatenate([jnp.where(sub == 0, x[:1], pltpu.roll(x[1:], 1, axis=1)), x[:1]], axis=0)


def primitives(q, rate):
    r = 1.0 / q[0]
    u = [q[1] * r, q[2] * r, q[3] * r]
    kin = 0.5 * (q[1] * u[0] + q[2] * u[1] + q[3] * u[2])
    p = GAMMA1 * (q[4] - kin)
    inv_t = q[0] / p
    e1 = DT * jnp.exp(rate - inv_t)
    e2 = (2.0 * DT) * jnp.exp(-1.5 * inv_t)
    return r, u, p, inv_t, e1, e2


def relax(kind):
    return jnp.where(kind == 1.0, 2.0 * DT, 0.0), jnp.where(kind == 2.0, DT, 0.0)


def forward_row(q, rate, kind, sub):
    _, u, p, _, e1, e2 = primitives(q, rate)
    ri, rs = relax(kind)
    w1 = e1 * q[5]
    w2 = e2 * q[6]
    hp = (0.5 * DT) * p
    ce = (1.0 - 12.0 * DT) - ri
    cm = ce - rs
    acc = [q[k] * (cm if k in (1, 2, 3) else ce) for k in range(8)]
    acc[0] = acc[0] + ri
    acc[1] = acc[1] + 0.8 * ri
    acc[4] = acc[4] + E0 * ri + (3.0 * w1 + 2.0 * w2)
    acc[5] = acc[5] + ri - w1
    acc[6] = acc[6] + (w1 - w2)
    acc[7] = acc[7] + w2
    radial = None
    for d in range(3):
        h = (0.5 * DT) * u[d]
        ha = h - 2.0 * DT
        hb = h + 2.0 * DT
        a = [q[k] * ha for k in range(8)]
        b = [q[k] * hb for k in range(8)]
        pu = hp * u[d]
        a[d + 1] = a[d + 1] + hp
        b[d + 1] = b[d + 1] + hp
        a[4] = a[4] + pu
        b[4] = b[4] + pu
        if d == 1:
            radial = (a, b)
        elif d == 0:
            acc = [acc[k] - axial_p(a[k], sub) + axial_m(b[k], sub) for k in range(8)]
        else:
            acc = [acc[k] - lane_p(a[k]) + lane_m(b[k]) for k in range(8)]
    return acc, radial[0], radial[1]


def adjoint_row(q, rate, kind, c, cp, cm, bz, sub, bax):
    r, u, p, inv_t, e1, e2 = primitives(q, rate)
    ri, rs = relax(kind)
    al1 = 3.0 * c[4] - c[5] + c[6]
    al2 = 2.0 * c[4] - c[6] + c[7]
    g1 = e1 * al1
    g2 = e2 * al2
    rate_grad = g1 * q[5]
    gg = (rate_grad + 1.5 * (g2 * q[6])) * inv_t
    ce = (1.0 - 12.0 * DT) - ri
    cmo = ce - rs
    out = [c[k] * (cmo if k in (1, 2, 3) else ce) for k in range(8)]
    out[5] = out[5] + g1
    out[6] = out[6] + g2
    gp = gg * inv_t * r
    rho = -gg * r
    total = [None] * 8
    for d in range(3):
        if d == 0:
            hi = [axial_p(c[k], sub) for k in range(8)]
            lo = [axial_m(c[k], sub) for k in range(8)]
            w = [(hi[k] - lo[k]) + bax * c[k] for k in range(8)]
        elif d == 1:
            hi, lo = cp, cm
            w = [(hi[k] - lo[k]) + bz * c[k] for k in range(8)]
        else:
            hi = [lane_p(c[k]) for k in range(8)]
            lo = [lane_m(c[k]) for k in range(8)]
            w = [hi[k] - lo[k] for k in range(8)]
        total = [hi[k] + lo[k] if total[k] is None else total[k] + (hi[k] + lo[k]) for k in range(8)]
        h = (0.5 * DT) * u[d]
        s = q[0] * w[0]
        for k in range(1, 8):
            s = s + q[k] * w[k]
        s = ((0.5 * DT) * r) * (s + p * w[4])
        out = [out[k] + h * w[k] for k in range(8)]
        out[d + 1] = out[d + 1] + s
        rho = rho - s * u[d]
        gp = gp + ((0.5 * DT) * w[d + 1] + h * w[4])
    gp = GAMMA1 * gp
    rho = rho + (0.5 * gp) * (u[0] * u[0] + u[1] * u[1] + u[2] * u[2])
    out[0] = out[0] + rho
    for j in range(3):
        out[j + 1] = out[j + 1] - gp * u[j]
    out[4] = out[4] + gp
    return [out[k] + (2.0 * DT) * total[k] for k in range(8)], rate_grad


def sub_index():
    return lax.broadcasted_iota(jnp.int32, (1, 8, 128), 1)


def axial_mend():
    t = lax.broadcasted_iota(jnp.int32, (2, 8, 128), 0)
    s = lax.broadcasted_iota(jnp.int32, (2, 8, 128), 1)
    return jnp.where((t == 1) & (s == 7), -2.0, jnp.where((t == 0) & (s == 0), 2.0, 0.0))


def radial_ends():
    pos = lax.axis_index("cross") * lax.axis_size("role") + lax.axis_index("role")
    count = lax.axis_size("cross") * lax.axis_size("role")
    first = R - 2 * pos
    last = R + 2 * (count - pos) - 1
    return first, last


def scalar_mend(j, first, last):
    return jnp.where(j == last, -2.0, jnp.where(j == first, 2.0, 0.0)).astype(F32)


def edge_rows(s):
    lane = iota_lane()
    pack = jnp.where(lane >= 2 * STRIDE, 2, jnp.where(lane >= STRIDE, 1, 0))
    return pack * SLOTS + s


def lane_between(a, b):
    lane = iota_lane()
    return (lane >= a) & (lane < b)


def build_kernel(x_ref, rate_ref, kind_ref, out_ref, pad_ref):
    rows = x_ref.shape[2]
    for f in range(NF):
        v = x_ref[f, 0] if f < 8 else (rate_ref[0] if f == 8 else kind_ref[0].astype(F32))
        pad_ref[f, R : R + rows] = v
        pad_ref[f, 0:R] = jnp.broadcast_to(v[0:1], (R, 128))
        pad_ref[f, R + rows : 2 * R + rows] = jnp.broadcast_to(v[rows - 1 : rows], (R, 128))
    for d in range(out_ref.shape[0]):
        for f in range(NF):
            out_ref[d, f * CHIP : (f + 1) * CHIP] = pad_ref[f, 4 * d : 4 * d + CHIP]


def spread_kernel(own_ref, other_ref, *refs):
    fa_refs, (s0_ref, f_ref, e_ref, fe_ref, left_ref, right_ref) = refs[: RF + 1], refs[RF + 1 :]
    role = lax.axis_index("role")

    def edges(v, j, own, sends):
        p, s = j // SLOTS, j % SLOTS
        base = STRIDE * p
        a = rl(v, base + HALO)
        b = rl(v, base + 3 * HALO - (128 - 2 * HALO))
        w = jnp.where(lane_between(base + HALO, base + 3 * HALO), a, b)
        own[s] = w if own[s] is None else jnp.where(lane_between(base + HALO, base + 5 * HALO), w, own[s])
        k = base + HALO * s
        mk = lane_between(k, k + HALO)
        for i, shift in enumerate((k, k + HALO - 128)):
            t = rl(v, shift)
            sends[i] = t if sends[i] is None else jnp.where(mk, t, sends[i])

    for f in range(NF):
        own, sends = [None] * SLOTS, [None, None]
        for j in range(NROW):
            rows = pl.ds(f * CHIP + j + 2 * role, 8, stride=BLK)
            a, b = own_ref[rows, :], other_ref[rows, :]
            v = jnp.stack([jnp.where(role == 0, a, b), jnp.where(role == 0, b, a)])
            s0_ref[f, j] = v
            edges(v, j, own, sends)
        for s in range(SLOTS):
            e_ref[f, s] = own[s]
        left_ref[f], right_ref[f] = sends
    for f in range(8):
        own, sends = [None] * SLOTS, [None, None]
        for i in range(NFA):
            src = fa_refs[i // 2]
            first = f * 32 + i % 2
            v = jnp.stack([src[pl.ds(first, 8, stride=4), :], src[pl.ds(first + 2, 8, stride=4), :]])
            f_ref[f, i] = v
            edges(v, i + R - RF, own, sends)
        for s in range(SLOTS):
            fe_ref[f, s] = own[s]
        left_ref[NF + f], right_ref[NF + f] = sends


def load(ref, j):
    return [ref[k, j] for k in range(8)]


def store(ref, j, v):
    for k in range(8):
        ref[k, j] = v[k]


def main_kernel(s0_ref, f_ref, out_ref, kg_ref, st_ref, a_ref, b_ref):
    sub, bax = sub_index(), axial_mend()
    first, last = radial_ends()

    def level(src, dst, lo, hi, mix):
        def one(j, _):
            acc, a, b = forward_row(load(src, j), s0_ref[8, j], s0_ref[9, j], sub)
            store(a_ref, j, a)
            store(b_ref, j, b)
            store(dst, j, acc)
            return 0

        def two(j, _):
            jp = jnp.where(j == last, j, j + 1)
            jm = jnp.where(j == first, j, j - 1)
            for k in range(8):
                v = dst[k, j] - a_ref[k, jp] + b_ref[k, jm]
                if mix:
                    v = 0.5 * s0_ref[k, j] + 0.5 * v
                dst[k, j] = v
            return 0

        lax.fori_loop(lo - 1, hi + 2, one, 0)
        lax.fori_loop(lo, hi + 1, two, 0)

    st1, st2, st3 = st_ref.at[0], st_ref.at[1], st_ref.at[2]
    level(s0_ref, st1, 1, NROW - 2, False)
    level(st1, st2, 2, NROW - 3, True)
    level(st2, st3, 3, NROW - 4, False)

    def back(state, c_ref, offset, j):
        jp = jnp.where(j == last, j, j + 1) - offset
        jm = jnp.where(j == first, j, j - 1) - offset
        return adjoint_row(
            load(state, j), s0_ref[8, j], s0_ref[9, j], load(c_ref, j - offset), load(c_ref, jp), load(c_ref, jm),
            scalar_mend(j, first, last), sub, bax,
        )

    foff = R - RF

    def adj3(j, _):
        o, g = back(st3, f_ref, foff, j)
        store(a_ref, j, [0.5 * v for v in o])
        st_ref[2, 0, j] = 0.5 * g
        return 0

    def adj2(j, _):
        o, g = back(st2, a_ref, 0, j)
        store(b_ref, j, [0.5 * f_ref[k, j - foff] + o[k] for k in range(8)])
        st_ref[2, 0, j] = st_ref[2, 0, j] + g
        return 0

    def adj1(j, _):
        o, g = back(st1, b_ref, 0, j)
        store(a_ref, j, [0.5 * v for v in o])
        st_ref[2, 0, j] = st_ref[2, 0, j] + 0.5 * g
        return 0

    def adj0(j, _):
        o, g = back(s0_ref, a_ref, 0, j)
        for k in range(8):
            out_ref[k, j - R] = 0.5 * b_ref[k, j] + o[k]
        kg_ref[j - R] = st_ref[2, 0, j] + g
        return 0

    lax.fori_loop(3, NROW - 3, adj3, 0)
    lax.fori_loop(4, NROW - 4, adj2, 0)
    lax.fori_loop(5, NROW - 5, adj1, 0)
    lax.fori_loop(6, NROW - 6, adj0, 0)


def wrap_slots(ref, k, s, v):
    ref[k, s + 1] = v
    if s == 0:
        ref[k, SLOTS + 1] = rl(v, -STRIDE)
    if s == SLOTS - 1:
        ref[k, 0] = rl(v, STRIDE)


def edge_mend(s, first, last):
    rows = edge_rows(s)
    return rows == first, rows == last


def edge_adjoint(state, e_ref, c_ref, s, first, last, sub, bax):
    mf, ml = edge_mend(s, first, last)
    c = load(c_ref, s + 1)
    cp = [jnp.where(ml, c[k], c_ref[k, s + 2]) for k in range(8)]
    cm = [jnp.where(mf, c[k], c_ref[k, s]) for k in range(8)]
    bz = jnp.where(ml, -2.0, jnp.where(mf, 2.0, 0.0))
    return adjoint_row(load(state, s), e_ref[8, s], e_ref[9, s], c, cp, cm, bz, sub, bax)


def edge_kernel(e_ref, fe_ref, fl_ref, fr_ref, om_ref, kg_ref, out_ref, rg_ref,
                e0_ref, st_ref, a_ref, b_ref, c_ref, fx_ref):
    sub, bax = sub_index(), axial_mend()
    first, last = radial_ends()

    def halo(v, f, s):
        l, r = rl(fl_ref[f], -HALO * s), rl(fr_ref[f], HALO * (5 - s))
        for p in range(3):
            base = STRIDE * p
            v = jnp.where(lane_between(base, base + HALO), l, v)
            v = jnp.where(lane_between(base + 5 * HALO, base + 6 * HALO), r, v)
        return v

    for f in range(NF):
        for s in range(SLOTS):
            e0_ref[f, s] = halo(e_ref[f, s], f, s)
    for f in range(8):
        for s in range(SLOTS):
            wrap_slots(fx_ref, f, s, halo(fe_ref[f, s], NF + f, s))

    def level(src, dst, mix):
        for s in range(SLOTS):
            acc, a, b = forward_row(load(src, s), e0_ref[8, s], e0_ref[9, s], sub)
            store(dst, s, acc)
            for k in range(8):
                wrap_slots(a_ref, k, s, a[k])
                wrap_slots(b_ref, k, s, b[k])
        for s in range(SLOTS):
            mf, ml = edge_mend(s, first, last)
            for k in range(8):
                ap = jnp.where(ml, a_ref[k, s + 1], a_ref[k, s + 2])
                bm = jnp.where(mf, b_ref[k, s + 1], b_ref[k, s])
                v = dst[k, s] - ap + bm
                if mix:
                    v = 0.5 * e0_ref[k, s] + 0.5 * v
                dst[k, s] = v

    st1, st2, st3 = st_ref.at[0], st_ref.at[1], st_ref.at[2]
    level(e0_ref, st1, False)
    level(st1, st2, True)
    level(st2, st3, False)

    def back(state, src, s):
        return edge_adjoint(state, e0_ref, src, s, first, last, sub, bax)

    c3_ref, c2_ref, c1_ref = a_ref, b_ref, c_ref
    grads = [None] * SLOTS
    for s in range(SLOTS):
        o, g = back(st3, fx_ref, s)
        for k in range(8):
            wrap_slots(c3_ref, k, s, 0.5 * o[k])
        grads[s] = 0.5 * g
    for s in range(SLOTS):
        o, g = back(st2, c3_ref, s)
        for k in range(8):
            wrap_slots(c2_ref, k, s, 0.5 * fx_ref[k, s + 1] + o[k])
        grads[s] = grads[s] + g
    for s in range(4):
        o, g = back(st1, c2_ref, s)
        for k in range(8):
            wrap_slots(c1_ref, k, s, 0.5 * o[k])
        grads[s] = grads[s] + 0.5 * g

    head = lane_between(0, HALO)
    tail = lane_between(128 - HALO, 128)

    def merge(m, e):
        return jnp.where(head, rl(e, -(STRIDE + HALO)), jnp.where(tail, rl(e, 128 - HALO - (STRIDE + 4 * HALO)), m))

    for r in range(2):
        s = (R + r) % SLOTS
        o, g = back(e0_ref, c1_ref, s)
        for k in range(8):
            v = merge(om_ref[k, r], 0.5 * c2_ref[k, s + 1] + o[k])
            out_ref[pl.ds(k * 32 + r, 8, stride=4), :] = v[0]
            out_ref[pl.ds(k * 32 + 2 + r, 8, stride=4), :] = v[1]
        v = merge(kg_ref[r], grads[s] + g)
        rg_ref[pl.ds(r, 8, stride=4), :] = v[0]
        rg_ref[pl.ds(2 + r, 8, stride=4), :] = v[1]


def call(kernel, outs, scratch, *args, near=True, leave=False):
    args = [pltpu.with_memory_space_constraint(a, pltpu.VMEM if near else pltpu.HBM) for a in args]
    return pl.pallas_call(
        kernel,
        out_shape=[jax.ShapeDtypeStruct(o, F32) if leave else pltpu.VMEM(o, F32) for o in outs],
        in_specs=[pl.BlockSpec(memory_space=pltpu.VMEM)] * len(args),
        out_specs=[pl.BlockSpec(memory_space=pltpu.VMEM)] * len(outs),
        scratch_shapes=[pltpu.VMEM(s, F32) for s in scratch],
        compiler_params=pltpu.CompilerParams(vmem_limit_bytes=14 * 1024 * 1024),
    )(*args)


T = (2, 8, 128)


def shifted(x, axis, step):
    n = lax.axis_size(axis)
    return lax.ppermute(x, axis, [(i, (i + step) % n) for i in range(n)])


def sections(checkpoint, rate, kinds, final_adjoint):
    chips = lax.axis_size("cross")
    rows = checkpoint.shape[2]
    fa = final_adjoint.reshape(256, 128)
    halo = {}
    for step in (-2, -1, 1, 2):
        halo[step] = shifted(fa, CR, -step)
    (send,) = call(
        build_kernel, [(chips, BLK, 128)], [(NF, rows + 2 * R, 128)], checkpoint, rate, kinds, near=False, leave=True
    )
    own = lax.all_to_all(send, "cross", split_axis=0, concat_axis=0, tiled=True)
    own = own.reshape(chips * BLK, 128)
    other = shifted(own, "role", 1)
    s0, f, e, fe, left, right = call(
        spread_kernel,
        [(NF, NROW) + T, (8, NFA) + T, (NF, SLOTS) + T, (8, SLOTS) + T, (NF + 8,) + T, (NF + 8,) + T],
        [],
        own, other, halo[-2], halo[-1], fa, halo[1], halo[2],
    )
    from_right = shifted(left, "azim", -1)
    from_left = shifted(right, "azim", 1)
    om, kg = call(
        main_kernel,
        [(8, 2) + T, (2,) + T],
        [(3, 8, NROW) + T, (8, NROW) + T, (8, NROW) + T],
        s0, f,
    )
    out, rg = call(
        edge_kernel,
        [(256, 128), (32, 128)],
        [(NF, SLOTS) + T, (3, 8, SLOTS) + T] + [(8, SLOTS + 2) + T] * 4,
        e, fe, from_left, from_right, om, kg, leave=True,
    )
    return out.reshape(8, 16, 2, 128), rg.reshape(16, 2, 128)


def solution(mesh):
    return jax.shard_map(
        sections,
        mesh=mesh,
        in_specs=(
            P(None, CR, None, "azim"),
            P(CR, None, "azim"),
            P(CR, None, "azim"),
            P(None, None, CR, "azim"),
        ),
        out_specs=(P(None, None, CR, "azim"), P(None, CR, "azim")),
        check_vma=False,
    )
```

time: 53.6 us -> 54.3 us (1.013)
  the two profiles are of different devices: /device:TPU:6 before, /device:TPU:1 now
where the time goes in v3:
time: 54.3 us; the launch traced here: 54.1 us
  blocking collectives  19 us (35%)
  Pallas kernels  14.6 us (27%)
  starting transfers between devices  11.1 us (20%)
  waiting for transfers between devices  8.6 us (16%)
  between operations  0.68 us (1%)
    all_to_all x1, blocking collectives, sections(): own = lax.all_to_all(send, 'cross', split_axis=0, concat_axis=0, tiled=True)  19 us
    pallas_call x4, Pallas kernels, call(): pl.pallas_call(kernel, out_shape=[jax.ShapeDtypeStruct(o, F32) if leave e...  14.6 us
    ppermute x7, starting transfers between devices, shifted(): return lax.ppermute(x, axis, [(i, (i + step) % n) for i in range(n)])  11.1 us
    ppermute x7, waiting for transfers between devices, shifted(): return lax.ppermute(x, axis, [(i, (i + step) % n) for i in range(n)])  8.6 us
  transfers between devices with their start and end apart: 7, of which 3 were waited for; matrix products, arithmetic and copies ran while one was open for 0% of the time, Pallas kernels for 13%

profile of v3, /device:TPU:1, one launch (start us, length us, event | category | flops | bytes accessed | tf_op | source)
XLA Modules:
  0.0 54.1 jit_solution(15969737519846933555)
XLA Ops:
  0.6 0.0 copy-start
  0.6 1.0 %shard_map.59 = f32[8,160,128]{2,1,0:T(8,128)S(1)} custom-call(f32[8,1,32,128]{3,2,1,0:T(8,128)} %x_ref.1, f32[1,32,128]{2,1,0:T(8,128)} %rate_ref.1, s32[1,32,128]{2,1,0:T(8,128)} %kind_ref.1), custom_call_target="tpu_custom_call" | custom-call | tf_op jit(solution)/shard_map/pallas_call | solution.py:420
  1.7 19.0 %all_to_all.5 = f32[8,160,128]{2,1,0:T(8,128)S(1)} all-to-all(f32[8,160,128]{2,1,0:T(8,128)S(1)} %shard_map.59), channel_id=1, replica_groups=mesh['azim'=16,'cross'=8,'role'=2] {'cross'}, dimensions={0} | all-to-all | bytes 1310720 | tf_op jit(solution)/shard_map/all_to_all | solution.py:448
  20.7 2.2 %collective-permute-start = (f32[1280,128]{1,0:T(8,128)S(1)}, f32[1280,128]{1,0:T(8,128)S(1)}, u32[]{:S(2)}, u32[]{:S(2)}) collective-permute-start(f32[1280,128]{1,0:T(8,128)S(1)} %bitcast.4), channel_id=1, source_target_pairs={{0,1},{1,0},{2,3},{3,2},{4,5},{5,4},{6,7},{7,6},{8,9},{9,8},{10,11... | collective-permute-start | bytes 1966088 | tf_op jit(solution)/shard_map/ppermute | solution.py:435
  22.9 0.0 copy-done
  22.9 1.2 %collective-permute-start.4 = (f32[256,128]{1,0:T(8,128)S(1)}, f32[256,128]{1,0:T(8,128)S(1)}, u32[]{:S(2)}, u32[]{:S(2)}) collective-permute-start(f32[256,128]{1,0:T(8,128)S(1)} %bitcast.6), channel_id=1, source_target_pairs={{0,14},{1,15},{2,0},{3,1},{4,2},{5,3},{6,4},{7,5},{8,6},{9,7},{10,... | collective-permute-start | bytes 393224 | tf_op jit(solution)/shard_map/ppermute | solution.py:435
  24.1 0.3 collective-permute-start.3
  24.3 1.5 %collective-permute-start.2 = (f32[256,128]{1,0:T(8,128)S(1)}, f32[256,128]{1,0:T(8,128)S(1)}, u32[]{:S(2)}, u32[]{:S(2)}) collective-permute-start(f32[256,128]{1,0:T(8,128)S(1)} %bitcast.8), channel_id=1, source_target_pairs={{0,1},{1,2},{2,3},{3,4},{4,5},{5,6},{6,7},{7,8},{8,9},{9,10},{10,1... | collective-permute-start | bytes 393224 | tf_op jit(solution)/shard_map/ppermute | solution.py:435
  25.8 0.3 collective-permute-start.1
  26.1 1.8 %collective-permute-done.4.refs_4_ = f32[256,128]{1,0:T(8,128)S(1)} collective-permute-done((f32[256,128]{1,0:T(8,128)S(1)}, f32[256,128]{1,0:T(8,128)S(1)}, u32[]{:S(2)}, u32[]{:S(2)}) %collective-permute-start.4) | collective-permute-done | bytes 131104 | tf_op jit(solution)/shard_map/ppermute | solution.py:435
  27.9 1.6 %collective-permute-done.3.refs_3_ = f32[256,128]{1,0:T(8,128)S(1)} collective-permute-done((f32[256,128]{1,0:T(8,128)S(1)}, f32[256,128]{1,0:T(8,128)S(1)}, u32[]{:S(2)}, u32[]{:S(2)}) %collective-permute-start.3) | collective-permute-done | bytes 131104 | tf_op jit(solution)/shard_map/ppermute | solution.py:435
  29.5 0.0 collective-permute-done.2.refs_1_
  29.5 5.2 %collective-permute-done.1.refs_0_ = f32[256,128]{1,0:T(8,128)S(1)} collective-permute-done((f32[256,128]{1,0:T(8,128)S(1)}, f32[256,128]{1,0:T(8,128)S(1)}, u32[]{:S(2)}, u32[]{:S(2)}) %collective-permute-start.1) | collective-permute-done | bytes 131104 | tf_op jit(solution)/shard_map/ppermute | solution.py:435
  34.7 0.0 collective-permute-done.other_ref
  34.7 1.7 %shard_map.60 = (f32[10,14,2,8,128]{4,3,2,1,0:T(8,128)S(1)}, f32[8,10,2,8,128]{4,3,2,1,0:T(8,128)S(1)}, f32[10,5,2,8,128]{4,3,2,1,0:T(8,128)S(1)}, f32[8,5,2,8,1...) custom-call(f32[1280,128]{1,0:T(8,128)S(1)} %bitcast.5, ...), custom_call_target="tpu_custom_call" | custom-call | tf_op jit(solution)/shard_map/pallas_call | solution.py:420
  36.4 1.7 %collective-permute-start.5 = (f32[18,2,8,128]{3,2,1,0:T(8,128)S(1)}, f32[18,2,8,128]{3,2,1,0:T(8,128)S(1)}, u32[]{:S(2)}, u32[]{:S(2)}) collective-permute-start(f32[18,2,8,128]{3,2,1,0:T(8,128)S(1)} %get-tuple-element.14), channel_id=1, source_target_pairs={{0,16},{16,32},{32,48},{48,64},{64,80},{80,96},{96,112},{112,128},... | collective-permute-start | bytes 442376 | tf_op jit(solution)/shard_map/ppermute | solution.py:435
  38.1 4.1 %collective-permute-start.6 = (f32[18,2,8,128]{3,2,1,0:T(8,128)S(1)}, f32[18,2,8,128]{3,2,1,0:T(8,128)S(1)}, u32[]{:S(2)}, u32[]{:S(2)}) collective-permute-start(f32[18,2,8,128]{3,2,1,0:T(8,128)S(1)} %get-tuple-element.15), channel_id=1, source_target_pairs={{0,240},{16,0},{32,16},{48,32},{64,48},{80,64},{96,80},{112,96},{1... | collective-permute-start | bytes 442376 | tf_op jit(solution)/shard_map/ppermute | solution.py:435
  42.2 7.1 %shard_map.61 = (f32[8,2,2,8,128]{4,3,2,1,0:T(8,128)S(1)}, f32[2,2,8,128]{3,2,1,0:T(8,128)S(1)}) custom-call(f32[10,14,2,8,128]{4,3,2,1,0:T(8,128)S(1)} %get-tuple-element.16.s0_ref, f32[8,10,2,8,128]{4,3,2,1,0:T(8,128)S(1)} %get-tuple-element.17.f_ref), custom_call_target="tpu_custom_call" | custom-call | tf_op jit(solution)/shard_map/pallas_call | solution.py:420
  49.2 0.0 collective-permute-done.5.fl_ref
  49.2 0.0 collective-permute-done.6.fr_ref
  49.3 4.9 %shard_map.62 = (f32[256,128]{1,0:T(8,128)}, f32[32,128]{1,0:T(8,128)}) custom-call(f32[10,5,2,8,128]{4,3,2,1,0:T(8,128)S(1)} %get-tuple-element.12.e_ref, f32[8,5,2,8,128]{4,3,2,1,0:T(8,128)S(1)} %get-tuple-element.13.fe_ref, f32[18,2,8,128]{3,2,1,0:T(8,128)S(1)} %collective-permute-done.5.fl_ref, f32[18,2,8,128]{3,2,1,0:T(8,128)S(1)} %collective-permute-done.6.fr_ref, ...), custom_call_target="tpu_custom_call" | custom-call | tf_op jit(solution)/shard_map/pallas_call | solution.py:420
Async XLA Ops:
  0.6 22.2 %copy-start = (f32[8,16,2,128]{3,2,1,0:T(2,128)S(1)}, f32[8,16,2,128]{3,2,1,0:T(2,128)}, u32[]{:S(2)}) copy-start(f32[8,16,2,128]{3,2,1,0:T(2,128)} %param.7) | copy-start | bytes 393220
  20.7 14.0 %collective-permute-start = (f32[1280,128]{1,0:T(8,128)S(1)}, f32[1280,128]{1,0:T(8,128)S(1)}, u32[]{:S(2)}, u32[]{:S(2)}) collective-permute-start(f32[1280,128]{1,0:T(8,128)S(1)} %bitcast.4), channel_id=1, source_target_pairs={{0,1},{1,0},{2,3},{3,2},{4,5},{5,4},{6,7},{7,6},{8,9},{9,8},{10,11... | collective-permute-start | bytes 1966088 | tf_op jit(solution)/shard_map/ppermute | solution.py:435
  22.9 5.1 %collective-permute-start.4 = (f32[256,128]{1,0:T(8,128)S(1)}, f32[256,128]{1,0:T(8,128)S(1)}, u32[]{:S(2)}, u32[]{:S(2)}) collective-permute-start(f32[256,128]{1,0:T(8,128)S(1)} %bitcast.6), channel_id=1, source_target_pairs={{0,14},{1,15},{2,0},{3,1},{4,2},{5,3},{6,4},{7,5},{8,6},{9,7},{10,... | collective-permute-start | bytes 393224 | tf_op jit(solution)/shard_map/ppermute | solution.py:435
  24.1 5.4 %collective-permute-start.3 = (f32[256,128]{1,0:T(8,128)S(1)}, f32[256,128]{1,0:T(8,128)S(1)}, u32[]{:S(2)}, u32[]{:S(2)}) collective-permute-start(f32[256,128]{1,0:T(8,128)S(1)} %bitcast.7), channel_id=1, source_target_pairs={{0,15},{1,0},{2,1},{3,2},{4,3},{5,4},{6,5},{7,6},{8,7},{9,8},{10,9... | collective-permute-start | bytes 393224 | tf_op jit(solution)/shard_map/ppermute | solution.py:435
  24.3 5.2 %collective-permute-start.2 = (f32[256,128]{1,0:T(8,128)S(1)}, f32[256,128]{1,0:T(8,128)S(1)}, u32[]{:S(2)}, u32[]{:S(2)}) collective-permute-start(f32[256,128]{1,0:T(8,128)S(1)} %bitcast.8), channel_id=1, source_target_pairs={{0,1},{1,2},{2,3},{3,4},{4,5},{5,6},{6,7},{7,8},{8,9},{9,10},{10,1... | collective-permute-start | bytes 393224 | tf_op jit(solution)/shard_map/ppermute | solution.py:435
  25.8 8.9 %collective-permute-start.1 = (f32[256,128]{1,0:T(8,128)S(1)}, f32[256,128]{1,0:T(8,128)S(1)}, u32[]{:S(2)}, u32[]{:S(2)}) collective-permute-start(f32[256,128]{1,0:T(8,128)S(1)} %bitcast.9), channel_id=1, source_target_pairs={{0,2},{1,3},{2,4},{3,5},{4,6},{5,7},{6,8},{7,9},{8,10},{9,11},{10,... | collective-permute-start | bytes 393224 | tf_op jit(solution)/shard_map/ppermute | solution.py:435
  36.4 12.9 %collective-permute-start.5 = (f32[18,2,8,128]{3,2,1,0:T(8,128)S(1)}, f32[18,2,8,128]{3,2,1,0:T(8,128)S(1)}, u32[]{:S(2)}, u32[]{:S(2)}) collective-permute-start(f32[18,2,8,128]{3,2,1,0:T(8,128)S(1)} %get-tuple-element.14), channel_id=1, source_target_pairs={{0,16},{16,32},{32,48},{48,64},{64,80},{80,96},{96,112},{112,128},... | collective-permute-start | bytes 442376 | tf_op jit(solution)/shard_map/ppermute | solution.py:435
  38.1 11.2 %collective-permute-start.6 = (f32[18,2,8,128]{3,2,1,0:T(8,128)S(1)}, f32[18,2,8,128]{3,2,1,0:T(8,128)S(1)}, u32[]{:S(2)}, u32[]{:S(2)}) collective-permute-start(f32[18,2,8,128]{3,2,1,0:T(8,128)S(1)} %get-tuple-element.15), channel_id=1, source_target_pairs={{0,240},{16,0},{32,16},{48,32},{64,48},{80,64},{96,80},{112,96},{1... | collective-permute-start | bytes 442376 | tf_op jit(solution)/shard_map/ppermute | solution.py:435

commit v4 on v3

--- a/solution.py
+++ b/solution.py
@@ -191,23 +191,43 @@
             out_ref[d, f * CHIP : (f + 1) * CHIP] = pad_ref[f, 4 * d : 4 * d + CHIP]
 
 
-def spread_kernel(own_ref, other_ref, *refs):
-    fa_refs, (s0_ref, f_ref, e_ref, fe_ref, left_ref, right_ref) = refs[: RF + 1], refs[RF + 1 :]
+def edge_parts(v, j, own, sends):
+    p, s = j // SLOTS, j % SLOTS
+    base = STRIDE * p
+    a = rl(v, base + HALO)
+    b = rl(v, base + 3 * HALO - (128 - 2 * HALO))
+    w = jnp.where(lane_between(base + HALO, base + 3 * HALO), a, b)
+    own[s] = w if own[s] is None else jnp.where(lane_between(base + HALO, base + 5 * HALO), w, own[s])
+    k = base + HALO * s
+    mk = lane_between(k, k + HALO)
+    for i, shift in enumerate((k, k + HALO - 128)):
+        t = rl(v, shift)
+        sends[i] = t if sends[i] is None else jnp.where(mk, t, sends[i])
+
+
+def adjoint_spread_kernel(own_ref, mate_ref, near_ref, far_ref, mates_ref, f_ref, fe_ref, left_ref, right_ref):
+    is_low = lax.axis_index("role") == 0
+    order = ((far_ref, mates_ref), (near_ref, mate_ref), (own_ref, None), (mate_ref, near_ref), (mates_ref, far_ref))
+
+    def pick(i, start):
+        low, high = order[i // 2]
+        v = low[pl.ds(start, 8, stride=4), :]
+        return v if high is None else jnp.where(is_low, v, high[pl.ds(start, 8, stride=4), :])
+
+    for f in range(8):
+        own, sends = [None] * SLOTS, [None, None]
+        for i in range(NFA):
+            first = f * 32 + i % 2
+            v = jnp.stack([pick(i, first), pick(i, first + 2)])
+            f_ref[f, i] = v
+            edge_parts(v, i + R - RF, own, sends)
+        for s in range(SLOTS):
+            fe_ref[f, s] = own[s]
+        left_ref[f], right_ref[f] = sends
+
+
+def spread_kernel(own_ref, other_ref, fl_ref, fr_ref, s0_ref, e_ref, left_ref, right_ref):
     role = lax.axis_index("role")
-
-    def edges(v, j, own, sends):
-        p, s = j // SLOTS, j % SLOTS
-        base = STRIDE * p
-        a = rl(v, base + HALO)
-        b = rl(v, base + 3 * HALO - (128 - 2 * HALO))
-        w = jnp.where(lane_between(base + HALO, base + 3 * HALO), a, b)
-        own[s] = w if own[s] is None else jnp.where(lane_between(base + HALO, base + 5 * HALO), w, own[s])
-        k = base + HALO * s
-        mk = lane_between(k, k + HALO)
-        for i, shift in enumerate((k, k + HALO - 128)):
-            t = rl(v, shift)
-            sends[i] = t if sends[i] is None else jnp.where(mk, t, sends[i])
-
     for f in range(NF):
         own, sends = [None] * SLOTS, [None, None]
         for j in range(NROW):
@@ -215,21 +235,13 @@
             a, b = own_ref[rows, :], other_ref[rows, :]
             v = jnp.stack([jnp.where(role == 0, a, b), jnp.where(role == 0, b, a)])
             s0_ref[f, j] = v
-            edges(v, j, own, sends)
+            edge_parts(v, j, own, sends)
         for s in range(SLOTS):
             e_ref[f, s] = own[s]
         left_ref[f], right_ref[f] = sends
     for f in range(8):
-        own, sends = [None] * SLOTS, [None, None]
-        for i in range(NFA):
-            src = fa_refs[i // 2]
-            first = f * 32 + i % 2
-            v = jnp.stack([src[pl.ds(first, 8, stride=4), :], src[pl.ds(first + 2, 8, stride=4), :]])
-            f_ref[f, i] = v
-            edges(v, i + R - RF, own, sends)
-        for s in range(SLOTS):
-            fe_ref[f, s] = own[s]
-        left_ref[NF + f], right_ref[NF + f] = sends
+        left_ref[NF + f] = fl_ref[f]
+        right_ref[NF + f] = fr_ref[f]
 
 
 def load(ref, j):
@@ -439,20 +451,29 @@
     chips = lax.axis_size("cross")
     rows = checkpoint.shape[2]
     fa = final_adjoint.reshape(256, 128)
-    halo = {}
-    for step in (-2, -1, 1, 2):
-        halo[step] = shifted(fa, CR, -step)
+    count = lax.axis_size(CR)
+    outward = [(i, (i + (2 if i % 2 == 0 else -2)) % count) for i in range(count)]
+    mate = shifted(fa, "role", 1)
+    far = lax.ppermute(fa, CR, outward)
+    near = lax.ppermute(mate, CR, outward)
+    mates = shifted(near, "role", 1)
     (send,) = call(
         build_kernel, [(chips, BLK, 128)], [(NF, rows + 2 * R, 128)], checkpoint, rate, kinds, near=False, leave=True
     )
     own = lax.all_to_all(send, "cross", split_axis=0, concat_axis=0, tiled=True)
     own = own.reshape(chips * BLK, 128)
     other = shifted(own, "role", 1)
-    s0, f, e, fe, left, right = call(
+    f, fe, fl, fr = call(
+        adjoint_spread_kernel,
+        [(8, NFA) + T, (8, SLOTS) + T, (8,) + T, (8,) + T],
+        [],
+        fa, mate, near, far, mates,
+    )
+    s0, e, left, right = call(
         spread_kernel,
-        [(NF, NROW) + T, (8, NFA) + T, (NF, SLOTS) + T, (8, SLOTS) + T, (NF + 8,) + T, (NF + 8,) + T],
+        [(NF, NROW) + T, (NF, SLOTS) + T, (NF + 8,) + T, (NF + 8,) + T],
         [],
-        own, other, halo[-2], halo[-1], fa, halo[1], halo[2],
+        own, other, fl, fr,
     )
     from_right = shifted(left, "azim", -1)
     from_left = shifted(right, "azim", 1)

time: 54.3 us -> 54.5 us (level)
  starting transfers between devices: 11.1 us -> 14.4 us
  waiting for transfers between devices: 8.6 us -> 5.43 us
    ppermute x7 -> x5, waiting for transfers between devices: 8.6 us -> 2.9 us  [shifted(): return lax.ppermute(x, axis, [(i, (i + step) % n) for i in range(n)])]
    ppermute x0 -> x2, waiting for transfers between devices: none -> 2.53 us  [the longest x1 2.53 us: sections(): near = lax.ppermute(mate, CR, outward)]
    ppermute x7 -> x5, starting transfers between devices: 11.1 us -> 13.1 us  [shifted(): return lax.ppermute(x, axis, [(i, (i + step) % n) for i in range(n)])]
    ppermute x0 -> x2, starting transfers between devices: none -> 1.29 us  [the longest x1 1.18 us: sections(): near = lax.ppermute(mate, CR, outward)]
    pallas_call x4 -> x5, Pallas kernels: 14.6 us -> 14.7 us  [call(): pl.pallas_call(kernel, out_shape=[jax.ShapeDtypeStruct(o, F32) if leave e...]
  transfers between devices with their start and end apart: 7 -> 7, of which waited for: 3 -> 3; matrix products, arithmetic and copies ran while one was open for 0% -> 0% of each run, Pallas kernels for 13% -> 14%
where the time goes in v4:
time: 54.5 us; the launch traced here: 54.3 us
  blocking collectives  19 us (35%)
  Pallas kernels  14.7 us (27%)
  starting transfers between devices  14.4 us (26%)
  waiting for transfers between devices  5.43 us (10%)
  between operations  0.7 us (1%)
    all_to_all x1, blocking collectives, sections(): own = lax.all_to_all(send, 'cross', split_axis=0, concat_axis=0, tiled=True)  19 us
    pallas_call x5, Pallas kernels, call(): pl.pallas_call(kernel, out_shape=[jax.ShapeDtypeStruct(o, F32) if leave e...  14.7 us
    ppermute x5, starting transfers between devices, shifted(): return lax.ppermute(x, axis, [(i, (i + step) % n) for i in range(n)])  13.1 us
    ppermute x5, waiting for transfers between devices, shifted(): return lax.ppermute(x, axis, [(i, (i + step) % n) for i in range(n)])  2.9 us
    ppermute x1, waiting for transfers between devices, sections(): near = lax.ppermute(mate, CR, outward)  2.53 us
    ppermute x1, starting transfers between devices, sections(): near = lax.ppermute(mate, CR, outward)  1.18 us
  transfers between devices with their start and end apart: 7, of which 3 were waited for; matrix products, arithmetic and copies ran while one was open for 0% of the time, Pallas kernels for 14%

profile of v4, /device:TPU:1, one launch (start us, length us, event | category | flops | bytes accessed | tf_op | source)
XLA Modules:
  0.0 54.3 jit_solution(4790491522740359020)
XLA Ops:
  0.6 0.0 copy-start
  0.6 1.0 %shard_map.59 = f32[8,160,128]{2,1,0:T(8,128)S(1)} custom-call(f32[8,1,32,128]{3,2,1,0:T(8,128)} %x_ref.1, f32[1,32,128]{2,1,0:T(8,128)} %rate_ref.1, s32[1,32,128]{2,1,0:T(8,128)} %kind_ref.1), custom_call_target="tpu_custom_call" | custom-call | tf_op jit(solution)/shard_map/pallas_call | solution.py:432
  1.7 19.0 %all_to_all.5 = f32[8,160,128]{2,1,0:T(8,128)S(1)} all-to-all(f32[8,160,128]{2,1,0:T(8,128)S(1)} %shard_map.59), channel_id=1, replica_groups=mesh['azim'=16,'cross'=8,'role'=2] {'cross'}, dimensions={0} | all-to-all | bytes 1310720 | tf_op jit(solution)/shard_map/all_to_all | solution.py:463
  20.7 2.2 %collective-permute-start = (f32[1280,128]{1,0:T(8,128)S(1)}, f32[1280,128]{1,0:T(8,128)S(1)}, u32[]{:S(2)}, u32[]{:S(2)}) collective-permute-start(f32[1280,128]{1,0:T(8,128)S(1)} %bitcast.4), channel_id=1, source_target_pairs={{0,1},{1,0},{2,3},{3,2},{4,5},{5,4},{6,7},{7,6},{8,9},{9,8},{10,11... | collective-permute-start | bytes 1966088 | tf_op jit(solution)/shard_map/ppermute | solution.py:447
  22.9 0.0 copy-done
  22.9 0.0 collective-permute-start.1
  22.9 1.9 %collective-permute-done.1.mate_ref = f32[256,128]{1,0:T(8,128)S(1)} collective-permute-done((f32[256,128]{1,0:T(8,128)S(1)}, f32[256,128]{1,0:T(8,128)S(1)}, u32[]{:S(2)}, u32[]{:S(2)}) %collective-permute-start.1) | collective-permute-done | bytes 131104 | tf_op jit(solution)/shard_map/ppermute | solution.py:447
  24.8 1.2 %collective-permute-start.2 = (f32[256,128]{1,0:T(8,128)S(1)}, f32[256,128]{1,0:T(8,128)S(1)}, u32[]{:S(2)}, u32[]{:S(2)}) collective-permute-start(f32[256,128]{1,0:T(8,128)S(1)} %collective-permute-done.1.mate_ref), channel_id=1, source_target_pairs={{0,2},{1,15},{2,4},{3,1},{4,6},{5,3},{6,8},{7,5},{8,10},{9,7},{10,... | collective-permute-start | bytes 393224 | tf_op jit(solution)/shard_map/ppermute | solution.py:458
  26.0 0.1 collective-permute-start.3
  26.1 2.5 %collective-permute-done.2.near_ref = f32[256,128]{1,0:T(8,128)S(1)} collective-permute-done((f32[256,128]{1,0:T(8,128)S(1)}, f32[256,128]{1,0:T(8,128)S(1)}, u32[]{:S(2)}, u32[]{:S(2)}) %collective-permute-start.2) | collective-permute-done | bytes 131104 | tf_op jit(solution)/shard_map/ppermute | solution.py:458
  28.6 5.1 %collective-permute-start.4 = (f32[256,128]{1,0:T(8,128)S(1)}, f32[256,128]{1,0:T(8,128)S(1)}, u32[]{:S(2)}, u32[]{:S(2)}) collective-permute-start(f32[256,128]{1,0:T(8,128)S(1)} %collective-permute-done.2.near_ref), channel_id=1, source_target_pairs={{0,1},{1,0},{2,3},{3,2},{4,5},{5,4},{6,7},{7,6},{8,9},{9,8},{10,11... | collective-permute-start | bytes 393224 | tf_op jit(solution)/shard_map/ppermute | solution.py:447
  33.7 0.0 collective-permute-done.3.far_ref
  33.7 1.0 %collective-permute-done.4.mates_ref = f32[256,128]{1,0:T(8,128)S(1)} collective-permute-done((f32[256,128]{1,0:T(8,128)S(1)}, f32[256,128]{1,0:T(8,128)S(1)}, u32[]{:S(2)}, u32[]{:S(2)}) %collective-permute-start.4) | collective-permute-done | bytes 131104 | tf_op jit(solution)/shard_map/ppermute | solution.py:447
  34.7 0.6 %shard_map.60 = (f32[8,10,2,8,128]{4,3,2,1,0:T(8,128)S(1)}, f32[8,5,2,8,128]{4,3,2,1,0:T(8,128)S(1)}, f32[8,2,8,128]{3,2,1,0:T(8,128)S(1)}, f32[8,2,8,128]{3,2,1,0:T(8,128)S(1)}) custom-call(f32[256,128]{1,0:T(8,128)S(1)} %bitcast.8, f32[256,128]{1,0:T(8,128)S(1)} %collective-permute-done.1.mate_ref, f32[256,128]{1,0:T(8,128)S(1)} %collective-permute-done.2.near_ref, ...), custom_call_target="tpu_custom_call" | custom-call | tf_op jit(solution)/shard_map/pallas_call | solution.py:432
  35.4 0.0 collective-permute-done.other_ref
  35.4 1.1 %shard_map.61 = (f32[10,14,2,8,128]{4,3,2,1,0:T(8,128)S(1)}, f32[10,5,2,8,128]{4,3,2,1,0:T(8,128)S(1)}, f32[18,2,8,128]{3,2,1,0:T(8,128)S(1)}, f32[18,2,8,128]{3,2,1,0:T(8,128)S(1)}) custom-call(f32[1280,128]{1,0:T(8,128)S(1)} %bitcast.5, f32[1280,128]{1,0:T(8,128)S(1)} %collective-permute-done.other_ref, f32[8,2,8,128]{3,2,1,0:T(8,128)S(1)} %get-tuple-element.14.fl_ref, ...), custom_call_target="tpu_custom_call" | custom-call | tf_op jit(solution)/shard_map/pallas_call | solution.py:432
  36.5 1.7 %collective-permute-start.5 = (f32[18,2,8,128]{3,2,1,0:T(8,128)S(1)}, f32[18,2,8,128]{3,2,1,0:T(8,128)S(1)}, u32[]{:S(2)}, u32[]{:S(2)}) collective-permute-start(f32[18,2,8,128]{3,2,1,0:T(8,128)S(1)} %get-tuple-element.18), channel_id=1, source_target_pairs={{0,16},{16,32},{32,48},{48,64},{64,80},{80,96},{96,112},{112,128},... | collective-permute-start | bytes 442376 | tf_op jit(solution)/shard_map/ppermute | solution.py:447
  38.2 4.1 %collective-permute-start.6 = (f32[18,2,8,128]{3,2,1,0:T(8,128)S(1)}, f32[18,2,8,128]{3,2,1,0:T(8,128)S(1)}, u32[]{:S(2)}, u32[]{:S(2)}) collective-permute-start(f32[18,2,8,128]{3,2,1,0:T(8,128)S(1)} %get-tuple-element.19), channel_id=1, source_target_pairs={{0,240},{16,0},{32,16},{48,32},{64,48},{80,64},{96,80},{112,96},{1... | collective-permute-start | bytes 442376 | tf_op jit(solution)/shard_map/ppermute | solution.py:447
  42.3 7.1 %shard_map.62 = (f32[8,2,2,8,128]{4,3,2,1,0:T(8,128)S(1)}, f32[2,2,8,128]{3,2,1,0:T(8,128)S(1)}) custom-call(f32[10,14,2,8,128]{4,3,2,1,0:T(8,128)S(1)} %get-tuple-element.20.s0_ref, f32[8,10,2,8,128]{4,3,2,1,0:T(8,128)S(1)} %get-tuple-element.21.f_ref), custom_call_target="tpu_custom_call" | custom-call | tf_op jit(solution)/shard_map/pallas_call | solution.py:432
  49.4 0.0 collective-permute-done.5.fl_ref
  49.4 0.0 collective-permute-done.6.fr_ref
  49.4 4.9 %shard_map.63 = (f32[256,128]{1,0:T(8,128)}, f32[32,128]{1,0:T(8,128)}) custom-call(f32[10,5,2,8,128]{4,3,2,1,0:T(8,128)S(1)} %get-tuple-element.16.e_ref, f32[8,5,2,8,128]{4,3,2,1,0:T(8,128)S(1)} %get-tuple-element.17.fe_ref, f32[18,2,8,128]{3,2,1,0:T(8,128)S(1)} %collective-permute-done.5.fl_ref, f32[18,2,8,128]{3,2,1,0:T(8,128)S(1)} %collective-permute-done.6.fr_ref, ...), custom_call_target="tpu_custom_call" | custom-call | tf_op jit(solution)/shard_map/pallas_call | solution.py:432
Async XLA Ops:
  0.6 22.2 %copy-start = (f32[8,16,2,128]{3,2,1,0:T(2,128)S(1)}, f32[8,16,2,128]{3,2,1,0:T(2,128)}, u32[]{:S(2)}) copy-start(f32[8,16,2,128]{3,2,1,0:T(2,128)} %param.7) | copy-start | bytes 393220
  20.7 14.7 %collective-permute-start = (f32[1280,128]{1,0:T(8,128)S(1)}, f32[1280,128]{1,0:T(8,128)S(1)}, u32[]{:S(2)}, u32[]{:S(2)}) collective-permute-start(f32[1280,128]{1,0:T(8,128)S(1)} %bitcast.4), channel_id=1, source_target_pairs={{0,1},{1,0},{2,3},{3,2},{4,5},{5,4},{6,7},{7,6},{8,9},{9,8},{10,11... | collective-permute-start | bytes 1966088 | tf_op jit(solution)/shard_map/ppermute | solution.py:447
  22.9 1.9 %collective-permute-start.1 = (f32[256,128]{1,0:T(8,128)S(1)}, f32[256,128]{1,0:T(8,128)S(1)}, u32[]{:S(2)}, u32[]{:S(2)}) collective-permute-start(f32[256,128]{1,0:T(8,128)S(1)} %bitcast.6), channel_id=1, source_target_pairs={{0,1},{1,0},{2,3},{3,2},{4,5},{5,4},{6,7},{7,6},{8,9},{9,8},{10,11... | collective-permute-start | bytes 393224 | tf_op jit(solution)/shard_map/ppermute | solution.py:447
  24.8 3.8 %collective-permute-start.2 = (f32[256,128]{1,0:T(8,128)S(1)}, f32[256,128]{1,0:T(8,128)S(1)}, u32[]{:S(2)}, u32[]{:S(2)}) collective-permute-start(f32[256,128]{1,0:T(8,128)S(1)} %collective-permute-done.1.mate_ref), channel_id=1, source_target_pairs={{0,2},{1,15},{2,4},{3,1},{4,6},{5,3},{6,8},{7,5},{8,10},{9,7},{10,... | collective-permute-start | bytes 393224 | tf_op jit(solution)/shard_map/ppermute | solution.py:458
  26.0 7.8 %collective-permute-start.3 = (f32[256,128]{1,0:T(8,128)S(1)}, f32[256,128]{1,0:T(8,128)S(1)}, u32[]{:S(2)}, u32[]{:S(2)}) collective-permute-start(f32[256,128]{1,0:T(8,128)S(1)} %bitcast.7), channel_id=1, source_target_pairs={{0,2},{1,15},{2,4},{3,1},{4,6},{5,3},{6,8},{7,5},{8,10},{9,7},{10,... | collective-permute-start | bytes 393224 | tf_op jit(solution)/shard_map/ppermute | solution.py:457
  28.6 6.1 %collective-permute-start.4 = (f32[256,128]{1,0:T(8,128)S(1)}, f32[256,128]{1,0:T(8,128)S(1)}, u32[]{:S(2)}, u32[]{:S(2)}) collective-permute-start(f32[256,128]{1,0:T(8,128)S(1)} %collective-permute-done.2.near_ref), channel_id=1, source_target_pairs={{0,1},{1,0},{2,3},{3,2},{4,5},{5,4},{6,7},{7,6},{8,9},{9,8},{10,11... | collective-permute-start | bytes 393224 | tf_op jit(solution)/shard_map/ppermute | solution.py:447
  36.5 12.9 %collective-permute-start.5 = (f32[18,2,8,128]{3,2,1,0:T(8,128)S(1)}, f32[18,2,8,128]{3,2,1,0:T(8,128)S(1)}, u32[]{:S(2)}, u32[]{:S(2)}) collective-permute-start(f32[18,2,8,128]{3,2,1,0:T(8,128)S(1)} %get-tuple-element.18), channel_id=1, source_target_pairs={{0,16},{16,32},{32,48},{48,64},{64,80},{80,96},{96,112},{112,128},... | collective-permute-start | bytes 442376 | tf_op jit(solution)/shard_map/ppermute | solution.py:447
  38.2 11.2 %collective-permute-start.6 = (f32[18,2,8,128]{3,2,1,0:T(8,128)S(1)}, f32[18,2,8,128]{3,2,1,0:T(8,128)S(1)}, u32[]{:S(2)}, u32[]{:S(2)}) collective-permute-start(f32[18,2,8,128]{3,2,1,0:T(8,128)S(1)} %get-tuple-element.19), channel_id=1, source_target_pairs={{0,240},{16,0},{32,16},{48,32},{64,48},{80,64},{96,80},{112,96},{1... | collective-permute-start | bytes 442376 | tf_op jit(solution)/shard_map/ppermute | solution.py:447
